TPU v7x, 32 devices: a whole 2x2x4 slice. The times are simulated.
32 devices in a mesh: gx: 4 (over y, core), gz: 4 (over z), grp: 2 (over x).
Axes of the slice: x: 2, y: 2, z: 4, core: 2. Of those that a mesh axis runs over, the one named last changes fastest.
Arguments:
- velocity: float32 [3, 3, 512, 2048], P(None, None, ('gz', 'grp'), 'gx'), may hold values from -5 to 5
- slab_average_downflow_speed: float32 [3], replicated, may hold values from 0.5 to 2
- mean_shear: float32 [3], replicated, may hold values from -2 to 2
- mode_counts: int32 [3, 2], replicated, may hold values from 64 to 128
Outputs:
- advanced: float32 [3, 3, 512, 2048], P(None, None, ('gz', 'grp'), 'gx')
- stress: float32 [6, 3, 512, 2048], P(None, None, ('gz', 'grp'), 'gx')
All inputs are finite; a program needn't handle non-finite values.
Results may differ from a plain program's by a relative error of at most 0.00015.
Values sent between devices are 32-bit elements; how exact they have to be, the bound alone decides.
A program may use at most 64 MiB of HBM per device.

v0:
```python
import math

import jax
import jax.numpy as jnp
from jax import lax
from jax.sharding import PartitionSpec as P

NX = 2048
NZ = 512
MODES = 256


molecular_diffusivity = 0.4
time_step = 0.2
highest = lax.Precision.HIGHEST
pair_first = (0, 0, 0, 1, 1, 2)
pair_second = (0, 1, 2, 1, 2, 2)


def with_halo(cells, sides, width):
    for axis, dim in sides:
        count = lax.axis_size(axis)
        head = lax.slice_in_dim(cells, 0, width, axis=dim)
        tail = lax.slice_in_dim(cells, cells.shape[dim] - width, cells.shape[dim], axis=dim)
        cells = jnp.concatenate(
            [
                lax.ppermute(tail, axis, [(i, (i + 1) % count) for i in range(count)]),
                cells,
                lax.ppermute(head, axis, [((i + 1) % count, i) for i in range(count)]),
            ],
            axis=dim,
        )
    return cells


def wave_numbers(modes):
    column = jnp.arange(modes, dtype=jnp.int32)
    half_modes = modes // 2
    return jnp.where(column < half_modes, column, column - half_modes + 1)


def wave_table(positions, length, modes):
    column = jnp.arange(modes, dtype=jnp.int32)
    numbers = wave_numbers(modes)
    phase_int = positions[:, None] * numbers[None, :] % length
    angles = phase_int.astype(jnp.float32) * jnp.float32(2.0 * math.pi / length)
    return jnp.where(column[None, :] < modes // 2, jnp.cos(angles), jnp.sin(angles))


def mode_weights(length, modes):
    column = jnp.arange(modes, dtype=jnp.int32)
    return jnp.where(column == 0, jnp.float32(1.0 / length), jnp.float32(2.0 / length))


def tendency_from(
    middle_entry,
    east_cells,
    west_cells,
    north_cells,
    south_cells,
    slab_average_downflow_speed,
    mean_shear,
):
    downflow_derivative_field = (east_cells - west_cells) * 0.5
    crossflow_derivative_field = (north_cells - south_cells) * 0.5
    diffusion_contribution = (
        east_cells + west_cells + north_cells + south_cells - 4.0 * middle_entry
    )
    holding_slab = slab_average_downflow_speed[:, None, None] + middle_entry[0]
    advanced_state = (
        -holding_slab[None] * downflow_derivative_field
        - middle_entry[2][None] * crossflow_derivative_field
        + molecular_diffusivity * diffusion_contribution
    )
    shear_term = mean_shear[:, None, None] * middle_entry[1]
    return jnp.concatenate([advanced_state[0:1] - shear_term[None], advanced_state[1:]], axis=0)


def runge_kutta(velocity, rate):
    first = velocity + time_step * rate(velocity)
    second = 0.75 * velocity + 0.25 * (first + time_step * rate(first))
    return velocity / 3.0 + 2.0 / 3.0 * (second + time_step * rate(second))


def with_products(components):
    products = [
        components[first_idx] * components[second_idx]
        for first_idx, second_idx in zip(pair_first, pair_second)
    ]
    return jnp.concatenate([components, jnp.stack(products)], axis=0)


def padded_rate(padded, slab_average_downflow_speed, mean_shear):
    return tendency_from(
        padded[:, :, 1:-1, 1:-1],
        padded[:, :, 1:-1, 2:],
        padded[:, :, 1:-1, :-2],
        padded[:, :, 2:, 1:-1],
        padded[:, :, :-2, 1:-1],
        slab_average_downflow_speed,
        mean_shear,
    )


def local(velocity, slab_average_downflow_speed, mean_shear, mode_counts):
    plane_count = velocity.shape[1]
    cells_z = velocity.shape[2]
    cells_x = velocity.shape[3]

    def rate(field):
        padded = with_halo(field, ((("gz", "grp"), 2), ("gx", 3)), 1)
        return padded_rate(padded, slab_average_downflow_speed, mean_shear)

    advanced = runge_kutta(velocity, rate)
    streamwise_devices = lax.axis_size("gx")
    spanwise_devices = lax.axis_size(("gz", "grp"))
    modes_x_local = MODES // streamwise_devices
    modes_z_local = MODES // spanwise_devices
    x_positions = lax.axis_index("gx") * cells_x + jnp.arange(cells_x, dtype=jnp.int32)
    z_positions = lax.axis_index(("gz", "grp")) * cells_z + jnp.arange(cells_z, dtype=jnp.int32)
    synth_x = wave_table(x_positions, NX, MODES)
    synth_z = wave_table(z_positions, NZ, MODES)
    tile_fields = with_products(advanced)
    analysis_x = synth_x * mode_weights(NX, MODES)[None, :]
    columns = analysis_x
    streamwise = lax.psum_scatter(
        jnp.einsum("fpzx,xm->mfpz", tile_fields, columns, precision=highest),
        "gx",
        scatter_dimension=0,
        tiled=True,
    )
    line_count = modes_x_local * 9 * plane_count
    per_device = -(-line_count // spanwise_devices)
    padded_count = per_device * spanwise_devices
    flat_lines = streamwise.reshape(line_count, cells_z)
    flat_lines = jnp.pad(flat_lines, ((0, padded_count - line_count), (0, 0)))
    zlines = lax.all_to_all(flat_lines, ("gz", "grp"), split_axis=0, concat_axis=1, tiled=True)
    whole_z = (
        wave_table(jnp.arange(NZ, dtype=jnp.int32), NZ, MODES) * mode_weights(NZ, MODES)[None, :]
    )
    zcoeffs = jnp.einsum("iz,zn->ni", zlines, whole_z, precision=highest)
    gathered = lax.all_to_all(zcoeffs, ("gz", "grp"), split_axis=0, concat_axis=1, tiled=True)
    spectral = gathered[:, :line_count].reshape(modes_z_local, modes_x_local, 9, plane_count)
    numbers = wave_numbers(MODES)
    z_modes = lax.axis_index(("gz", "grp")) * modes_z_local + jnp.arange(
        modes_z_local, dtype=jnp.int32
    )
    x_modes = lax.axis_index("gx") * modes_x_local + jnp.arange(modes_x_local, dtype=jnp.int32)
    keep_z = jnp.take(numbers, z_modes)[:, None] <= mode_counts[:, 1][None, :]
    keep_x = jnp.take(numbers, x_modes)[:, None] <= mode_counts[:, 0][None, :]
    keep = (keep_z[:, None, :] & keep_x[None, :, :]).astype(jnp.float32)
    spectral = spectral * keep[:, :, None, :]
    columns = synth_z
    partial_sum = jnp.einsum(
        "nmfp,zn->mfpz",
        lax.all_gather(spectral, ("gz", "grp"), axis=0, tiled=True),
        columns,
        precision=highest,
    )
    columns = synth_x
    filtered = jnp.einsum(
        "mfpz,xm->fpzx",
        lax.all_gather(partial_sum, "gx", axis=0, tiled=True),
        columns,
        precision=highest,
    )
    stresses = [
        filtered[3 + index] - filtered[first_idx] * filtered[second_idx]
        for index, (first_idx, second_idx) in enumerate(zip(pair_first, pair_second))
    ]
    return (advanced, jnp.stack(stresses))


def solution(mesh):
    return jax.shard_map(
        local,
        mesh=mesh,
        in_specs=(P(None, None, ("gz", "grp"), "gx"), P(), P(), P()),
        out_specs=(P(None, None, ("gz", "grp"), "gx"), P(None, None, ("gz", "grp"), "gx")),
        check_vma=False,
    )
```

profile of v0, /device:TPU:0, one launch (start us, length us, event | category | flops | bytes accessed | tf_op | source)
XLA Modules:
  0.0 299.1 jit_solution(3138307370650989517)
XLA Ops:
  7.2 1.1 fusion.98
  8.3 3.0 %collective-permute-start = (f32[3,3,1,512]{3,2,1,0:T(1,128)S(1)}, f32[3,3,1,512]{3,2,1,0:T(1,128)S(1)}, u32[]{:S(2)}, u32[]{:S(2)}) collective-permute-start(f32[3,3,1,512]{3,2,1,0:T(1,128)S(1)} %get-tuple-element.20), channel_id=1, source_target_pairs={{0,1},{1,2},{2,3},{3,4},{4,5},{5,6},{6,7},{7,0},{8,9},{9,10},{10,1... | collective-permute-start | bytes 55304 | tf_op jit(solution)/shard_map/ppermute | solution.py:27
  11.3 3.1 %collective-permute-start.1 = (f32[3,3,1,512]{3,2,1,0:T(1,128)S(1)}, f32[3,3,1,512]{3,2,1,0:T(1,128)S(1)}, u32[]{:S(2)}, u32[]{:S(2)}) collective-permute-start(f32[3,3,1,512]{3,2,1,0:T(1,128)S(1)} %get-tuple-element.21), channel_id=1, source_target_pairs={{1,0},{2,1},{3,2},{4,3},{5,4},{6,5},{7,6},{0,7},{9,8},{10,9},{11,1... | collective-permute-start | bytes 55304 | tf_op jit(solution)/shard_map/ppermute | solution.py:29
  14.4 1.2 multiply_bitcast_fusion.1
  15.7 0.4 collective-permute-done
  16.1 0.2 pad_maximum_fusion.30
  16.4 1.7 collective-permute-start.2
  18.1 6.3 %collective-permute-done.3 = f32[3,3,66,1]{3,2,1,0:T(8,128)S(1)} collective-permute-done((f32[3,3,66,1]{3,2,1,0:T(8,128)S(1)}, f32[3,3,66,1]{3,2,1,0:T(8,128)S(1)}, u32[]{:S(2)}, u32[]{:S(2)}) %collective-permute-start.3) | collective-permute-done | bytes 2408 | tf_op jit(solution)/shard_map/ppermute | solution.py:27
  24.5 1.2 collective-permute-done.2
  25.7 1.2 multiply_add_fusion.2
  27.0 0.6 copy-done.4
  27.5 0.1 slice_subtract_fusion.6
  27.6 0.3 fusion.2
  28.0 1.3 collective-permute-start.4
  29.3 3.5 %collective-permute-start.5 = (f32[3,3,1,512]{3,2,1,0:T(1,128)S(1)}, f32[3,3,1,512]{3,2,1,0:T(1,128)S(1)}, u32[]{:S(2)}, u32[]{:S(2)}) collective-permute-start(f32[3,3,1,512]{3,2,1,0:T(1,128)S(1)} %get-tuple-element.17), channel_id=1, source_target_pairs={{1,0},{2,1},{3,2},{4,3},{5,4},{6,5},{7,6},{0,7},{9,8},{10,9},{11,1... | collective-permute-start | bytes 55304 | tf_op jit(solution)/shard_map/ppermute | solution.py:29
  32.8 1.8 collective-permute-done.4
  34.6 0.2 pad_maximum_fusion.27
  34.8 0.1 collective-permute-start.7
  35.0 1.7 collective-permute-start.6
  36.6 0.1 fusion.46
  36.7 6.2 %collective-permute-done.7 = f32[3,3,66,1]{3,2,1,0:T(8,128)S(1)} collective-permute-done((f32[3,3,66,1]{3,2,1,0:T(8,128)S(1)}, f32[3,3,66,1]{3,2,1,0:T(8,128)S(1)}, u32[]{:S(2)}, u32[]{:S(2)}) %collective-permute-start.7) | collective-permute-done | bytes 2408 | tf_op jit(solution)/shard_map/ppermute | solution.py:27
  43.0 1.2 collective-permute-done.6
  44.2 1.2 multiply_add_fusion.1
  45.4 0.1 fusion.42
  45.6 0.4 fusion.5
  46.1 4.8 %collective-permute-start.9 = (f32[3,3,1,512]{3,2,1,0:T(1,128)S(1)}, f32[3,3,1,512]{3,2,1,0:T(1,128)S(1)}, u32[]{:S(2)}, u32[]{:S(2)}) collective-permute-start(f32[3,3,1,512]{3,2,1,0:T(1,128)S(1)} %get-tuple-element.13), channel_id=1, source_target_pairs={{1,0},{2,1},{3,2},{4,3},{5,4},{6,5},{7,6},{0,7},{9,8},{10,9},{11,1... | collective-permute-start | bytes 55304 | tf_op jit(solution)/shard_map/ppermute | solution.py:29
  50.9 1.7 collective-permute-done.8
  52.6 0.2 pad_maximum_fusion.24
  52.8 2.0 collective-permute-start.10
  54.8 0.1 fusion.41
  55.0 5.4 %collective-permute-done.11 = f32[3,3,66,1]{3,2,1,0:T(8,128)S(1)} collective-permute-done((f32[3,3,66,1]{3,2,1,0:T(8,128)S(1)}, f32[3,3,66,1]{3,2,1,0:T(8,128)S(1)}, u32[]{:S(2)}, u32[]{:S(2)}) %collective-permute-start.11) | collective-permute-done | bytes 2408 | tf_op jit(solution)/shard_map/ppermute | solution.py:27
  60.4 2.0 collective-permute-done.10
  62.4 1.2 multiply_add_fusion
  63.6 0.1 fusion.37
  63.8 0.4 constant_dynamic-update-slice_fusion
  64.5 0.7 copy-done.1
  65.3 15.9 %fusion.16 = f32[256,9,3,64]{3,0,2,1:T(8,128)} fusion(f32[9,3,64,512]{3,2,1,0:T(8,128)S(1)} %multiply_dynamic-update-slice_fusion, f32[256]{0:T(256)S(1)} %compare_select_fusion.4, s32[256]{0:T(256)S(1)} %add_select_fusion.4, s32[512]{0:T(512)S(1)} %iota_add_fusion, pred[256]{0:T(512)(128)(4,1)S(1)} %iota_compare_fusion), kind=kOutput, calls=%fused_computation.57 | convolution fusion | flops 2720006144 | bytes 5312768 | tf_op jit(solution)/shard_map/fpzx,xm->mfpz/dot_general | solution.py:127
  81.3 0.8 gather_fusion.1
  82.1 0.7 gather_fusion
  82.8 40.7 %reduce-scatter.2.cloned.1.call-done = f32[64,9,3,64]{3,0,2,1:T(8,128)} async-done(((f32[256,9,3,64]{3,0,2,1:T(8,128)}), f32[64,9,3,64]{3,0,2,1:T(8,128)}) %reduce-scatter.2.cloned.1.call-update) | async-done | bytes 442384 | tf_op jit(solution)/shard_map/reduce_scatter | solution.py:126
  123.5 1.8 copy.13
  125.3 0.4 all_to_all.24
  125.7 1.1 copy.14
  126.8 5.5 %all-to-all-start = ((f32[8,216,64]{1,2,0:T(8,128)}), f32[8,216,64]{1,2,0:T(8,128)S(1)}, u32[]{:S(2)}, u32[]{:S(2)}) async-start(f32[8,216,64]{1,2,0:T(8,128)} %copy.14), calls=%async_computation.1 | async-start | bytes 1048576 | tf_op jit(solution)/shard_map/all_to_all | solution.py:137
  132.4 0.1 broadcast_compare_fusion
  132.5 14.2 %all-to-all-done = f32[8,216,64]{1,2,0:T(8,128)S(1)} async-done(((f32[8,216,64]{1,2,0:T(8,128)}), f32[8,216,64]{1,2,0:T(8,128)S(1)}, u32[]{:S(2)}, u32[]{:S(2)}) %all-to-all-start) | async-done | bytes 442400 | tf_op jit(solution)/shard_map/all_to_all | solution.py:137
  146.7 4.6 %fusion.18 = f32[8,32,216]{2,1,0:T(8,128)} fusion(f32[216,512,1]{0,1,2:T(8,128)S(1)} %bitcast.48, f32[8,32]{1,0:T(8,128)S(1)} %fusion.76, s32[8,32]{1,0:T(8,128)S(1)} %add_select_fusion.3, pred[8,32]{1,0:T(8,128)(4,1)S(1)} %fusion.75), kind=kOutput, calls=%fused_computation.59 | convolution fusion | flops 341835776 | bytes 665856 | tf_op jit(solution)/shard_map/iz,zn->ni/dot_general | solution.py:141
  151.3 3.6 %all-to-all-start.1 = ((f32[8,32,216]{2,1,0:T(8,128)}), f32[8,32,216]{2,1,0:T(8,128)S(1)}, u32[]{:S(2)}, u32[]{:S(2)}) async-start(f32[8,32,216]{2,1,0:T(8,128)} %fusion.18), calls=%async_computation.2 | async-start | bytes 524288 | tf_op jit(solution)/shard_map/all_to_all | solution.py:142
  155.1 0.1 and_convert_fusion
  155.2 8.8 %all-to-all-done.1 = f32[8,32,216]{2,1,0:T(8,128)S(1)} async-done(((f32[8,32,216]{2,1,0:T(8,128)}), f32[8,32,216]{2,1,0:T(8,128)S(1)}, u32[]{:S(2)}, u32[]{:S(2)}) %all-to-all-start.1) | async-done | bytes 221216 | tf_op jit(solution)/shard_map/all_to_all | solution.py:142
  164.0 0.3 copy.16
  164.3 0.4 reshape.244
  164.7 0.3 broadcast_multiply_fusion
  164.9 1.1 copy.17
  166.0 0.2 all-gather.5.cloned.1.call-start
  166.3 62.6 %all-gather.3.cloned.1.call-done = f32[256,64,9,3]{1,0,3,2:T(8,128)} async-done(((f32[32,64,9,3]{1,0,3,2:T(8,128)}), f32[256,64,9,3]{1,0,3,2:T(8,128)}) %all-gather.3.cloned.1.call-update) | async-done | bytes 1769488 | tf_op jit(solution)/shard_map/all_gather | solution.py:156
  228.8 7.8 %fusion.58 = f32[64,9,3,64]{3,0,2,1:T(8,128)S(1)} fusion(f32[256,64,9,3]{1,0,3,2:T(8,128)} %all-gather.3.cloned.1.call-done, s32[256]{0:T(256)S(1)} %add_select_fusion.4, s32[64]{0:T(128)S(1)} %iota_add_fusion.1, pred[256]{0:T(512)(128)(4,1)S(1)} %iota_compare_fusion), kind=kOutput, calls=%fused_computation.133 | convolution fusion | flops 339984384 | bytes 2213376 | tf_op jit(solution)/shard_map/nmfp,zn->mfpz/dot_general | solution.py:154
  236.7 1.6 copy.18
  238.3 36.3 %all-gather.5.cloned.1.call-done = f32[256,9,3,64]{3,2,1,0:T(4,128)} async-done(((f32[64,9,3,64]{3,2,1,0:T(4,128)}), f32[256,9,3,64]{3,2,1,0:T(4,128)}) %all-gather.5.cloned.1.call-update) | async-done | bytes 1769488 | tf_op jit(solution)/shard_map/all_gather | solution.py:163
  274.6 15.7 %fusion = f32[9,3,64,512]{3,2,1,0:T(8,128)S(1)} fusion(f32[256,9,3,64]{3,2,1,0:T(4,128)} %all-gather.5.cloned.1.call-done, s32[256]{0:T(256)S(1)} %add_select_fusion.4, s32[512]{0:T(512)S(1)} %iota_add_fusion, pred[256]{0:T(512)(128)(4,1)S(1)} %iota_compare_fusion), kind=kOutput, calls=%fused_computation.2 | convolution fusion | flops 2719875072 | bytes 5311744 | tf_op jit(solution)/shard_map/mfpz,xm->fpzx/dot_general | solution.py:161
  290.5 0.1 fusion.35
  290.6 0.1 fusion.34
  290.8 0.1 fusion.32
  290.9 1.4 copy-done.2
  (49 shorter events, 1.2 us)
Async XLA Ops:
  7.2 9.0 %copy-start = (f32[3,3,64,512]{3,2,1,0:T(8,128)S(1)}, f32[3,3,64,512]{3,2,1,0:T(8,128)}, u32[]{:S(2)}) copy-start(f32[3,3,64,512]{3,2,1,0:T(8,128)} %param.4) | copy-start | bytes 3538948
  7.2 116.3 %reduce-scatter.2.cloned.1.call-start = ((), (), s32[]{:S(2)}) async-start(), calls=%async_computation.3 | async-start | bytes 4423680 | tf_op jit(solution)/shard_map/reduce_scatter | solution.py:126
  8.3 7.8 %collective-permute-start = (f32[3,3,1,512]{3,2,1,0:T(1,128)S(1)}, f32[3,3,1,512]{3,2,1,0:T(1,128)S(1)}, u32[]{:S(2)}, u32[]{:S(2)}) collective-permute-start(f32[3,3,1,512]{3,2,1,0:T(1,128)S(1)} %get-tuple-element.20), channel_id=1, source_target_pairs={{0,1},{1,2},{2,3},{3,4},{4,5},{5,6},{6,7},{7,0},{8,9},{9,10},{10,1... | collective-permute-start | bytes 55304 | tf_op jit(solution)/shard_map/ppermute | solution.py:27
  11.3 4.8 %collective-permute-start.1 = (f32[3,3,1,512]{3,2,1,0:T(1,128)S(1)}, f32[3,3,1,512]{3,2,1,0:T(1,128)S(1)}, u32[]{:S(2)}, u32[]{:S(2)}) collective-permute-start(f32[3,3,1,512]{3,2,1,0:T(1,128)S(1)} %get-tuple-element.21), channel_id=1, source_target_pairs={{1,0},{2,1},{3,2},{4,3},{5,4},{6,5},{7,6},{0,7},{9,8},{10,9},{11,1... | collective-permute-start | bytes 55304 | tf_op jit(solution)/shard_map/ppermute | solution.py:29
  16.3 8.1 %collective-permute-start.3 = (f32[3,3,66,1]{3,2,1,0:T(8,128)S(1)}, f32[3,3,66,1]{3,2,1,0:T(8,128)S(1)}, u32[]{:S(2)}, u32[]{:S(2)}) collective-permute-start(f32[3,3,66,1]{3,2,1,0:T(8,128)S(1)} %get-tuple-element.8), channel_id=1, source_target_pairs={{0,8},{8,16},{16,24},{24,0},{1,9},{9,17},{17,25},{25,1},{2,10},{10... | collective-permute-start | bytes 7136 | tf_op jit(solution)/shard_map/ppermute | solution.py:27
  16.4 9.3 %collective-permute-start.2 = (f32[3,3,66,1]{3,2,1,0:T(8,128)S(1)}, f32[3,3,66,1]{3,2,1,0:T(8,128)S(1)}, u32[]{:S(2)}, u32[]{:S(2)}) collective-permute-start(f32[3,3,66,1]{3,2,1,0:T(8,128)S(1)} %get-tuple-element.9), channel_id=1, source_target_pairs={{8,0},{16,8},{24,16},{0,24},{9,1},{17,9},{25,17},{1,25},{10,2},{18... | collective-permute-start | bytes 7136 | tf_op jit(solution)/shard_map/ppermute | solution.py:29
  26.9 0.7 copy-start.4
  27.9 8.7 %copy-start.3 = (f32[3]{0:T(128)S(1)}, f32[3]{0:T(128)}, u32[]{:S(2)}) copy-start(f32[3]{0:T(128)} %param.5) | copy-start | bytes 40
  28.0 6.7 %collective-permute-start.4 = (f32[3,3,1,512]{3,2,1,0:T(1,128)S(1)}, f32[3,3,1,512]{3,2,1,0:T(1,128)S(1)}, u32[]{:S(2)}, u32[]{:S(2)}) collective-permute-start(f32[3,3,1,512]{3,2,1,0:T(1,128)S(1)} %get-tuple-element.16), channel_id=1, source_target_pairs={{0,1},{1,2},{2,3},{3,4},{4,5},{5,6},{6,7},{7,0},{8,9},{9,10},{10,1... | collective-permute-start | bytes 55304 | tf_op jit(solution)/shard_map/ppermute | solution.py:27
  29.3 5.4 %collective-permute-start.5 = (f32[3,3,1,512]{3,2,1,0:T(1,128)S(1)}, f32[3,3,1,512]{3,2,1,0:T(1,128)S(1)}, u32[]{:S(2)}, u32[]{:S(2)}) collective-permute-start(f32[3,3,1,512]{3,2,1,0:T(1,128)S(1)} %get-tuple-element.17), channel_id=1, source_target_pairs={{1,0},{2,1},{3,2},{4,3},{5,4},{6,5},{7,6},{0,7},{9,8},{10,9},{11,1... | collective-permute-start | bytes 55304 | tf_op jit(solution)/shard_map/ppermute | solution.py:29
  34.8 8.1 %collective-permute-start.7 = (f32[3,3,66,1]{3,2,1,0:T(8,128)S(1)}, f32[3,3,66,1]{3,2,1,0:T(8,128)S(1)}, u32[]{:S(2)}, u32[]{:S(2)}) collective-permute-start(f32[3,3,66,1]{3,2,1,0:T(8,128)S(1)} %get-tuple-element.6), channel_id=1, source_target_pairs={{0,8},{8,16},{16,24},{24,0},{1,9},{9,17},{17,25},{25,1},{2,10},{10... | collective-permute-start | bytes 7136 | tf_op jit(solution)/shard_map/ppermute | solution.py:27
  35.0 9.2 %collective-permute-start.6 = (f32[3,3,66,1]{3,2,1,0:T(8,128)S(1)}, f32[3,3,66,1]{3,2,1,0:T(8,128)S(1)}, u32[]{:S(2)}, u32[]{:S(2)}) collective-permute-start(f32[3,3,66,1]{3,2,1,0:T(8,128)S(1)} %get-tuple-element.7), channel_id=1, source_target_pairs={{8,0},{16,8},{24,16},{0,24},{9,1},{17,9},{25,17},{1,25},{10,2},{18... | collective-permute-start | bytes 7136 | tf_op jit(solution)/shard_map/ppermute | solution.py:29
  46.1 6.5 %collective-permute-start.8 = (f32[3,3,1,512]{3,2,1,0:T(1,128)S(1)}, f32[3,3,1,512]{3,2,1,0:T(1,128)S(1)}, u32[]{:S(2)}, u32[]{:S(2)}) collective-permute-start(f32[3,3,1,512]{3,2,1,0:T(1,128)S(1)} %get-tuple-element.12), channel_id=1, source_target_pairs={{0,1},{1,2},{2,3},{3,4},{4,5},{5,6},{6,7},{7,0},{8,9},{9,10},{10,1... | collective-permute-start | bytes 55304 | tf_op jit(solution)/shard_map/ppermute | solution.py:27
  46.1 6.5 %collective-permute-start.9 = (f32[3,3,1,512]{3,2,1,0:T(1,128)S(1)}, f32[3,3,1,512]{3,2,1,0:T(1,128)S(1)}, u32[]{:S(2)}, u32[]{:S(2)}) collective-permute-start(f32[3,3,1,512]{3,2,1,0:T(1,128)S(1)} %get-tuple-element.13), channel_id=1, source_target_pairs={{1,0},{2,1},{3,2},{4,3},{5,4},{6,5},{7,6},{0,7},{9,8},{10,9},{11,1... | collective-permute-start | bytes 55304 | tf_op jit(solution)/shard_map/ppermute | solution.py:29
  52.8 7.6 %collective-permute-start.11 = (f32[3,3,66,1]{3,2,1,0:T(8,128)S(1)}, f32[3,3,66,1]{3,2,1,0:T(8,128)S(1)}, u32[]{:S(2)}, u32[]{:S(2)}) collective-permute-start(f32[3,3,66,1]{3,2,1,0:T(8,128)S(1)} %get-tuple-element.4), channel_id=1, source_target_pairs={{0,8},{8,16},{16,24},{24,0},{1,9},{9,17},{17,25},{25,1},{2,10},{10... | collective-permute-start | bytes 7136 | tf_op jit(solution)/shard_map/ppermute | solution.py:27
  52.8 9.6 %collective-permute-start.10 = (f32[3,3,66,1]{3,2,1,0:T(8,128)S(1)}, f32[3,3,66,1]{3,2,1,0:T(8,128)S(1)}, u32[]{:S(2)}, u32[]{:S(2)}) collective-permute-start(f32[3,3,66,1]{3,2,1,0:T(8,128)S(1)} %get-tuple-element.5), channel_id=1, source_target_pairs={{8,0},{16,8},{24,16},{0,24},{9,1},{17,9},{25,17},{1,25},{10,2},{18... | collective-permute-start | bytes 7136 | tf_op jit(solution)/shard_map/ppermute | solution.py:29
  64.2 1.0 copy-start.1
  125.7 6.6 %copy-start.5 = (s32[3,2]{0,1:T(2,128)S(1)}, s32[3,2]{0,1:T(2,128)}, u32[]{:S(2)}) copy-start(s32[3,2]{0,1:T(2,128)} %param.7) | copy-start | bytes 76
  126.8 19.8 %all-to-all-start = ((f32[8,216,64]{1,2,0:T(8,128)}), f32[8,216,64]{1,2,0:T(8,128)S(1)}, u32[]{:S(2)}, u32[]{:S(2)}) async-start(f32[8,216,64]{1,2,0:T(8,128)} %copy.14), calls=%async_computation.1 | async-start | bytes 1048576 | tf_op jit(solution)/shard_map/all_to_all | solution.py:137
  151.3 12.7 %all-to-all-start.1 = ((f32[8,32,216]{2,1,0:T(8,128)}), f32[8,32,216]{2,1,0:T(8,128)S(1)}, u32[]{:S(2)}, u32[]{:S(2)}) async-start(f32[8,32,216]{2,1,0:T(8,128)} %fusion.18), calls=%async_computation.2 | async-start | bytes 524288 | tf_op jit(solution)/shard_map/all_to_all | solution.py:142
  154.9 73.9 %all-gather.3.cloned.1.call-start = ((), (), s32[]{:S(2)}) async-start(), calls=%async_computation.4 | async-start | bytes 3981312 | tf_op jit(solution)/shard_map/all_gather | solution.py:156
  166.0 108.6 %all-gather.5.cloned.1.call-start = ((), (), s32[]{:S(2)}) async-start(), calls=%async_computation.5 | async-start | bytes 5898240 | tf_op jit(solution)/shard_map/all_gather | solution.py:163
  290.9 1.4 copy-start.2
Sparse Core Ops, SparseCore 0:
  81.3 42.1 reduce-scatter.1
  166.1 62.6 all-gather.2
  238.4 36.1 all-gather.4
where the time goes:
time: 304 us; the launch traced here: 299 us
  waiting for transfers between devices  189 us (62%)
  matrix products  44.1 us (15%)
  starting transfers between devices  30.9 us (10%)
  between operations  14.4 us (5%)
  local copies, waits for them, and re-layouts  12.2 us (4%)
  other arithmetic  8.34 us (3%)
    all_gather x1, waiting for transfers between devices, local(): lax.all_gather(spectral, ('gz', 'grp'), axis=0, tiled=True)  62.6 us
    reduce_scatter x1, waiting for transfers between devices, local(): lax.psum_scatter(jnp.einsum('fpzx,xm->mfpz', tile_fields, columns, precis...  40.7 us
    all_gather x1, waiting for transfers between devices, local(): lax.all_gather(partial_sum, 'gx', axis=0, tiled=True)  36.3 us
    ppermute x6, waiting for transfers between devices, with_halo(): lax.ppermute(tail, axis, [(i, (i + 1) % count) for i in range(count)])  21.9 us
    ppermute x6, starting transfers between devices, with_halo(): lax.ppermute(head, axis, [((i + 1) % count, i) for i in range(count)])  16.8 us
    dot_general x1, matrix products, local(): jnp.einsum('fpzx,xm->mfpz', tile_fields, columns, precision=highest)  15.9 us
    dot_general x1, matrix products, local(): jnp.einsum('mfpz,xm->fpzx', lax.all_gather(partial_sum, 'gx', axis=0, til...  15.7 us
    all_to_all x1, waiting for transfers between devices, local(): lax.all_to_all(flat_lines, ('gz', 'grp'), split_axis=0, concat_axis=1, ti...  14.2 us
  transfers between devices with their start and end apart: 17, of which 14 were waited for; matrix products, arithmetic and copies ran while one was open for 1% of the time, Pallas kernels for 0%

commit v1 on v0

v1 whole, which is shorter than its diff:
```python
import functools
import math

import jax
import jax.numpy as jnp
import numpy as np
from jax import lax
from jax.experimental import pallas as pl
from jax.experimental.pallas import tpu as pltpu
from jax.sharding import PartitionSpec as P

MODES = 256
FIELDS = 9
MESH = pl.DeviceIdType.MESH
ROWS = 8
LANES = 128

molecular_diffusivity = 0.4
time_step = 0.2
pair_first = (0, 0, 0, 1, 1, 2)
pair_second = (0, 1, 2, 1, 2, 2)
f32 = jnp.float32
bf16 = jnp.bfloat16


def wave_table(length):
    column = np.arange(MODES)
    half = MODES // 2
    numbers = np.where(column < half, column, column - half + 1)
    angles = (np.arange(length)[:, None] * numbers[None, :] % length) * (2.0 * math.pi / length)
    return np.where(column[None, :] < half, np.cos(angles), np.sin(angles)).astype(np.float32)


def split_table(table):
    high = table.astype(bf16)
    low = (table - high.astype(np.float32)).astype(bf16)
    return high, low


def split(values):
    high = values.astype(bf16)
    return high, (values - high.astype(f32)).astype(bf16)


def dot3(a, b, contract=((1,), (0,))):
    def one(x, y):
        return lax.dot_general(x, y, (contract, ((), ())), preferred_element_type=f32)

    return one(a[0], b[0]) + (one(a[0], b[1]) + one(a[1], b[0]))


def tendency_from(middle, east, west, north, south, slab, shear):
    downflow = (east - west) * 0.5
    crossflow = (north - south) * 0.5
    diffusion = east + west + north + south - 4.0 * middle
    holding = slab[:, None, None] + middle[0]
    state = (
        -holding[None] * downflow - middle[2][None] * crossflow + molecular_diffusivity * diffusion
    )
    return jnp.concatenate([state[0:1] - (shear[:, None, None] * middle[1])[None], state[1:]], axis=0)


def rate(padded, slab, shear):
    return tendency_from(
        padded[:, :, 1:-1, 1:-1],
        padded[:, :, 1:-1, 2:],
        padded[:, :, 1:-1, :-2],
        padded[:, :, 2:, 1:-1],
        padded[:, :, :-2, 1:-1],
        slab,
        shear,
    )


def inner(cells, width):
    return cells[:, :, width:-width, width:-width]


def runge_kutta(padded, slab, shear):
    first = inner(padded, 1) + time_step * rate(padded, slab, shear)
    second = 0.75 * inner(padded, 2) + 0.25 * (
        inner(first, 1) + time_step * rate(first, slab, shear)
    )
    return inner(padded, 3) / 3.0 + 2.0 / 3.0 * (
        inner(second, 1) + time_step * rate(second, slab, shear)
    )


def halo_kernel(sizes, v_ref, out_ref, send_sem, recv_sem, local_sem):
    gx_n, gz_n, grp_n = sizes
    z_n = gz_n * grp_n
    _, cz, cx = v_ref.shape
    gx = lax.axis_index("gx")
    z = lax.axis_index("gz") * grp_n + lax.axis_index("grp")
    steps = [(dx, dz) for dx in (-1, 0, 1) for dz in (-1, 0, 1) if dx or dz]

    def device(dx, dz):
        to_z = lax.rem(z + dz + z_n, z_n)
        return {
            "gx": lax.rem(gx + dx + gx_n, gx_n),
            "gz": lax.div(to_z, grp_n),
            "grp": lax.rem(to_z, grp_n),
        }

    barrier = pltpu.get_barrier_semaphore()
    for dx, dz in steps:
        pl.semaphore_signal(barrier, inc=1, device_id=device(dx, dz), device_id_type=MESH)
    pl.semaphore_wait(barrier, len(steps))
    source_x = {1: pl.ds(cx - LANES, LANES), -1: pl.ds(0, LANES), 0: pl.ds(0, cx)}
    target_x = {1: pl.ds(0, LANES), -1: pl.ds(LANES + cx, LANES), 0: pl.ds(LANES, cx)}
    source_z = {1: pl.ds(cz - ROWS, ROWS), -1: pl.ds(0, ROWS), 0: pl.ds(0, cz)}
    target_z = {1: pl.ds(0, ROWS), -1: pl.ds(ROWS + cz, ROWS), 0: pl.ds(ROWS, cz)}
    copies = []
    for index, (dx, dz) in enumerate(steps):
        copy = pltpu.make_async_remote_copy(
            src_ref=v_ref.at[:, source_z[dz], source_x[dx]],
            dst_ref=out_ref.at[:, target_z[dz], target_x[dx]],
            send_sem=send_sem.at[index],
            recv_sem=recv_sem.at[index],
            device_id=device(dx, dz),
            device_id_type=MESH,
        )
        copy.start()
        copies.append(copy)
    own = pltpu.make_async_copy(v_ref, out_ref.at[:, target_z[0], target_x[0]], local_sem)
    own.start()
    own.wait()
    for copy in copies:
        copy.wait()


def with_halo(velocity, sizes):
    count, cz, cx = velocity.shape
    return pl.pallas_call(
        functools.partial(halo_kernel, sizes),
        out_shape=jax.ShapeDtypeStruct((count, cz + 2 * ROWS, cx + 2 * LANES), f32),
        in_specs=[pl.BlockSpec(memory_space=pltpu.VMEM)],
        out_specs=pl.BlockSpec(memory_space=pl.ANY),
        scratch_shapes=[
            pltpu.SemaphoreType.DMA((8,)),
            pltpu.SemaphoreType.DMA((8,)),
            pltpu.SemaphoreType.DMA,
        ],
        compiler_params=pltpu.CompilerParams(collective_id=0, has_side_effects=True),
        name="halo",
    )(velocity)


def filter_kernel(
    sizes, planes, adv_ref, counts_ref, txh_hbm, txl_hbm, tzh_ref, tzl_ref, tth_ref, ttl_ref, out_ref,
    high, low, txh, txl, part_send, part_keep, part_recv, y_send, y_recv, z_send, z_recv, z_out, gath,
    table_sem, ps_sem, pr_sem, ys_sem, yr_sem, zs_sem, zr_sem, os_sem, gr_sem, gy_sem, gp_sem,
):
    gx_n, gz_n, grp_n = sizes
    z_n = gz_n * grp_n
    y_n = gx_n // 2
    units = gath.shape[0] // gx_n
    _, cz, cx = adv_ref.shape
    gx = lax.axis_index("gx")
    z = lax.axis_index("gz") * grp_n + lax.axis_index("grp")
    y, core = lax.div(gx, 2), lax.rem(gx, 2)
    other = 1 - core

    def at_x(to_y, to_core):
        return {"gx": 2 * to_y + to_core, "gz": lax.axis_index("gz"), "grp": lax.axis_index("grp")}

    def at_z(to_z):
        to_z = jnp.int32(to_z)
        return {"gx": gx, "gz": lax.div(to_z, grp_n), "grp": lax.rem(to_z, grp_n)}

    def remote(src, dst, send, recv, device):
        return pltpu.make_async_remote_copy(
            src_ref=src, dst_ref=dst, send_sem=send, recv_sem=recv, device_id=device, device_id_type=MESH
        )

    barrier = pltpu.get_barrier_semaphore()
    friends = [at_x(y, other)]
    friends += [at_x(lax.rem(y + d, y_n), core) for d in range(1, y_n)]
    friends += [at_z(lax.rem(z + d, z_n)) for d in range(1, z_n)]
    for friend in friends:
        pl.semaphore_signal(barrier, inc=1, device_id=friend, device_id_type=MESH)

    mine = pl.ds(pl.multiple_of(gx * cx, cx), cx)
    tables = [
        pltpu.make_async_copy(txh_hbm.at[mine, :], txh, table_sem.at[0]),
        pltpu.make_async_copy(txl_hbm.at[mine, :], txl, table_sem.at[1]),
    ]
    for copy in tables:
        copy.start()

    def put(unit, values):
        h, l = split(values)
        high[unit] = h
        low[unit] = l

    def prepare(p, carry):
        parts = [adv_ref[i * planes + p] for i in range(3)]
        for i in range(3):
            put(p * FIELDS + i, parts[i])
        for q, (a, b) in enumerate(zip(pair_first, pair_second)):
            put(p * FIELDS + 3 + q, parts[a] * parts[b])
        return carry

    lax.fori_loop(0, planes, prepare, 0)
    for unit in range(planes * FIELDS, gath.shape[0]):
        high[unit] = jnp.zeros((cz, cx), bf16)
        low[unit] = jnp.zeros((cz, cx), bf16)
    for copy in tables:
        copy.wait()
    pl.semaphore_wait(barrier, len(friends))

    def analyse(block):
        chosen = pl.ds(block * units, units)
        rows = (high[chosen].reshape(units * cz, cx), low[chosen].reshape(units * cz, cx))
        return dot3(rows, (txh[...], txl[...])).reshape(units, cz, MODES)

    order = list(range(1, y_n)) + [0]
    to_partner = [
        remote(part_send.at[d], part_recv.at[d], ps_sem.at[d], pr_sem.at[d], at_x(y, other))
        for d in range(y_n)
    ]
    for d in order:
        part_send[d] = analyse(2 * lax.rem(y + d, y_n) + other)
        to_partner[d].start()
    for d in order:
        part_keep[d] = analyse(2 * lax.rem(y + d, y_n) + core)
    to_y = {
        d: remote(
            y_send.at[d - 1], y_recv.at[d - 1], ys_sem.at[d - 1], yr_sem.at[d - 1],
            at_x(lax.rem(y + d, y_n), core),
        )
        for d in range(1, y_n)
    }
    for d in range(1, y_n):
        to_partner[d].wait_recv()
        y_send[d - 1] = part_keep[d] + part_recv[d]
        to_y[d].start()
    to_partner[0].wait_recv()
    for d in range(1, y_n):
        to_y[d].wait_recv()

    def forward(k, device_slot):
        return remote(z_send.at[k], z_recv.at[z], zs_sem.at[k], zr_sem.at[device_slot], at_z(k))

    for k in range(units):
        total = part_keep[0, k] + part_recv[0, k]
        for d in range(1, y_n):
            total = total + y_recv[d - 1, k]
        z_send[k] = total

        @pl.when(z != k)
        def _():
            forward(k, z).start()

        @pl.when(z == k)
        def _():
            z_recv[z] = total

    unit = gx * units + z

    def back(s, slot):
        return remote(z_out.at[s], gath.at[slot], os_sem.at[s], gr_sem.at[slot], at_z(s))

    @pl.when(z < units)
    def _():
        for s in range(z_n):

            @pl.when(z != s)
            def _():
                remote(z_send.at[0], z_recv.at[s], zs_sem.at[0], zr_sem.at[s], at_z(s)).wait_recv()

        plane = jnp.minimum(lax.div(unit, FIELDS), planes - 1)
        limit_x, limit_z = counts_ref[plane, 0], counts_ref[plane, 1]

        def numbers(axis):
            column = lax.broadcasted_iota(jnp.int32, (MODES, MODES), axis)
            half = MODES // 2
            return jnp.where(column < half, column, column - half + 1), column

        def weights(column, length):
            return jnp.where(column == 0, f32(1.0 / length), f32(2.0 / length))

        kz, nz = numbers(0)
        kx, nx = numbers(1)
        scale = weights(nz, z_n * cz) * weights(nx, gx_n * cx)
        scale = jnp.where((kz <= limit_z) & (kx <= limit_x), scale, 0.0)
        lines = split(z_recv[...].reshape(z_n * cz, MODES))
        spectral = dot3((tth_ref[...], ttl_ref[...]), lines) * scale
        z_out[...] = dot3((tzh_ref[...], tzl_ref[...]), split(spectral)).reshape(z_n, cz, MODES)
        for s in range(z_n):

            @pl.when(z != s)
            def _():
                back(s, unit).start()

            @pl.when(z == s)
            def _():
                gath[unit] = z_out[s]

    def spread(slot, k, d):
        return remote(
            gath.at[slot], gath.at[slot], gy_sem.at[d - 1, k], gr_sem.at[slot],
            at_x(lax.rem(y + d, y_n), core),
        )

    def share(slot, d, k):
        return remote(gath.at[slot], gath.at[slot], gp_sem.at[d, k], gr_sem.at[slot], at_x(y, other))

    for k in range(units):
        slot = gx * units + k

        @pl.when(z != k)
        def _():
            back(0, slot).wait_recv()

        for d in range(1, y_n):
            spread(slot, k, d).start()
        share(slot, 0, k).start()
    for d in range(1, y_n):
        for k in range(units):
            slot = (2 * lax.rem(y + d, y_n) + core) * units + k
            back(0, slot).wait_recv()
            share(slot, d, k).start()
    for d in range(y_n):
        for k in range(units):
            back(0, (2 * lax.rem(y + d, y_n) + other) * units + k).wait_recv()

    def synthesise(p, carry):
        rows = split(gath[pl.ds(p * FIELDS, FIELDS)].reshape(FIELDS * cz, MODES))
        filtered = dot3(rows, (txh[...], txl[...]), ((1,), (1,))).reshape(FIELDS, cz, cx)
        for q, (a, b) in enumerate(zip(pair_first, pair_second)):
            out_ref[q * planes + p] = filtered[3 + q] - filtered[a] * filtered[b]
        return carry

    lax.fori_loop(0, planes, synthesise, 0)

    for d in range(y_n):
        to_partner[d].wait_send()
    for d in range(1, y_n):
        to_y[d].wait_send()
    for k in range(units):

        @pl.when(z != k)
        def _():
            forward(k, z).wait_send()

        for d in range(1, y_n):
            spread(gx * units + k, k, d).wait_send()
        for d in range(y_n):
            share(gx * units + k, d, k).wait_send()

    @pl.when(z < units)
    def _():
        for s in range(z_n):

            @pl.when(z != s)
            def _():
                back(s, unit).wait_send()


def filtered_stress(advanced, mode_counts, sizes):
    gx_n, gz_n, grp_n = sizes
    z_n = gz_n * grp_n
    y_n = gx_n // 2
    count, cz, cx = advanced.shape
    planes = count // 3
    units = -(-FIELDS * planes // gx_n)
    assert gx_n % 2 == 0 and units <= z_n
    txh, txl = split_table(wave_table(cx * gx_n))
    table_z = wave_table(cz * z_n)
    tzh, tzl = split_table(table_z)
    tth, ttl = split_table(table_z.T)
    dma = pltpu.SemaphoreType.DMA
    vmem = pl.BlockSpec(memory_space=pltpu.VMEM)
    anywhere = pl.BlockSpec(memory_space=pl.ANY)
    others = max(y_n - 1, 1)
    total = gx_n * units
    return pl.pallas_call(
        functools.partial(filter_kernel, sizes, planes),
        out_shape=jax.ShapeDtypeStruct((6 * planes, cz, cx), f32),
        in_specs=[vmem, pl.BlockSpec(memory_space=pltpu.SMEM), anywhere, anywhere, vmem, vmem, vmem, vmem],
        out_specs=vmem,
        scratch_shapes=[
            pltpu.VMEM((total, cz, cx), bf16),
            pltpu.VMEM((total, cz, cx), bf16),
            pltpu.VMEM((cx, MODES), bf16),
            pltpu.VMEM((cx, MODES), bf16),
            pltpu.VMEM((y_n, units, cz, MODES), f32),
            pltpu.VMEM((y_n, units, cz, MODES), f32),
            pltpu.VMEM((y_n, units, cz, MODES), f32),
            pltpu.VMEM((others, units, cz, MODES), f32),
            pltpu.VMEM((others, units, cz, MODES), f32),
            pltpu.VMEM((units, cz, MODES), f32),
            pltpu.VMEM((z_n, cz, MODES), f32),
            pltpu.VMEM((z_n, cz, MODES), f32),
            pltpu.VMEM((total, cz, MODES), f32),
            dma((2,)),
            dma((y_n,)),
            dma((y_n,)),
            dma((others,)),
            dma((others,)),
            dma((units,)),
            dma((z_n,)),
            dma((z_n,)),
            dma((total,)),
            dma((others, units)),
            dma((y_n, units)),
        ],
        compiler_params=pltpu.CompilerParams(collective_id=1, has_side_effects=True),
        name="filter",
    )(advanced, mode_counts, *(jnp.asarray(t) for t in (txh, txl, tzh, tzl, tth, ttl)))


def local(sizes, velocity, slab, shear, mode_counts):
    three, planes, cz, cx = velocity.shape
    padded = with_halo(velocity.reshape(three * planes, cz, cx), sizes)
    padded = padded.reshape(three, planes, cz + 2 * ROWS, cx + 2 * LANES)
    padded = padded[:, :, ROWS - 3 : ROWS + cz + 3, LANES - 3 : LANES + cx + 3]
    advanced = runge_kutta(padded, slab, shear)
    stress = filtered_stress(advanced.reshape(three * planes, cz, cx), mode_counts, sizes)
    return advanced, stress.reshape(6, planes, cz, cx)


def solution(mesh):
    sizes = (mesh.shape["gx"], mesh.shape["gz"], mesh.shape["grp"])
    spread = P(None, None, ("gz", "grp"), "gx")
    return jax.shard_map(
        functools.partial(local, sizes),
        mesh=mesh,
        in_specs=(spread, P(), P(), P()),
        out_specs=(spread, spread),
        check_vma=False,
    )
```

time: 304 us -> 88.1 us (0.29)
  the two profiles are of different devices: /device:TPU:0 before, /device:TPU:31 now
where the time goes in v1:
time: 88.1 us; the launch traced here: 87.9 us
  Pallas kernels  70.7 us (80%)
  other arithmetic  12 us (14%)
  local copies, waits for them, and re-layouts  4.42 us (5%)
    pallas_call x1, Pallas kernels, filtered_stress(): pl.pallas_call(functools.partial(filter_kernel, sizes, planes), out_shape...  56.7 us
    pallas_call x1, Pallas kernels, with_halo(): pl.pallas_call(functools.partial(halo_kernel, sizes), out_shape=jax.Shape...  14 us
    add x3, other arithmetic, tendency_from(): -holding[None] * downflow - middle[2][None] * crossflow  5.54 us
    unnamed x10, local copies, waits for them, and re-layouts  4.2 us
    mul x3, other arithmetic, tendency_from(): -holding[None] * downflow - middle[2][None] * crossflow  2.58 us

profile of v1, /device:TPU:31, one launch (start us, length us, event | category | flops | bytes accessed | tf_op | source)
XLA Modules:
  0.0 87.9 jit_solution(3583130608770007563)
XLA Ops:
  0.6 0.0 copy-start.1
  0.6 14.0 %halo.1 = f32[9,80,768]{2,1,0:T(8,128)} custom-call(f32[9,64,512]{2,1,0:T(8,128)} %bitcast.24), custom_call_target="tpu_custom_call" | custom-call | tf_op jit(solution)/shard_map/halo/pallas_call | solution.py:134
  14.6 0.0 copy-start
  14.7 0.0 copy-done.1
  14.7 1.9 %fusion.16 = (f32[3,68,516]{2,1,0:T(8,128)S(1)}, f32[3,68,516]{2,1,0:T(8,128)S(1)}) fusion(f32[3,3,80,768]{3,2,1,0:T(8,128)} %bitcast.16, f32[3]{0:T(128)S(1)} %copy-done.1), kind=kLoop, calls=%fused_computation.30 | loop fusion | flops 421056 | bytes 1684236 | tf_op jit(solution)/shard_map/mul | solution.py:58
  16.6 0.2 copy-done
  16.7 0.0 copy-start.2
  16.7 2.4 %multiply_add_fusion.1 = f32[3,3,68,516]{3,2,1,0:T(8,128)S(1)} fusion(f32[3,3,80,768]{3,2,1,0:T(8,128)S(1)} %bitcast.17, f32[3,68,516]{2,1,0:T(8,128)S(1)} %get-tuple-element.3, f32[3,68,516]{2,1,0:T(8,128)S(1)} %get-tuple-element.2), kind=kLoop, calls=%fused_computation.8 | loop fusion | flops 3789504 | bytes 8421120 | tf_op jit(solution)/shard_map/add | solution.py:58
  19.1 0.0 copy-done.2
  19.1 0.2 fusion.12
  19.3 0.1 slice.159
  19.4 0.6 fusion.1
  20.0 0.4 fusion.11
  20.4 1.9 %multiply_add_fusion = f32[3,3,66,514]{3,2,1,0:T(8,128)S(1)} fusion(f32[3,3,68,516]{3,2,1,0:T(8,128)S(1)} %fusion.1, f32[3,66,514]{2,1,0:T(8,128)S(1)} %get-tuple-element.7, f32[3,66,514]{2,1,0:T(8,128)S(1)} %get-tuple-element.6), kind=kLoop, calls=%fused_computation.7 | loop fusion | flops 3663792 | bytes 8141760 | tf_op jit(solution)/shard_map/add | solution.py:58
  22.2 0.2 fusion.7
  22.4 0.1 slice.169
  22.5 1.3 %fusion = f32[3,3,66,514]{3,2,1,0:T(8,128)S(1)} fusion(f32[3,3,80,768]{3,2,1,0:T(8,128)S(1)} %bitcast.20, f32[2,3,66,514]{3,2,1,0:T(8,128)S(1)} %slice.169, f32[1,3,66,514]{3,2,1,0:T(8,128)S(1)} %fusion.7, f32[3,3,68,516]{3,2,1,0:T(8,128)S(1)} %fusion.1), kind=kLoop, calls=%fused_computation.1 | loop fusion | flops 1831896 | bytes 4885056 | tf_op jit(solution)/shard_map/add | solution.py:81
  23.8 0.3 fusion.21
  24.1 1.3 %multiply_add_fusion.2 = f32[3,3,64,512]{3,2,1,0:T(8,128)S(1)} fusion(f32[3,3,66,514]{3,2,1,0:T(8,128)S(1)} %fusion, f32[3,64,512]{2,1,0:T(8,128)S(1)} %get-tuple-element.5, f32[3,64,512]{2,1,0:T(8,128)S(1)} %get-tuple-element.4), kind=kLoop, calls=%fused_computation.14 | loop fusion | flops 3538944 | bytes 7864320 | tf_op jit(solution)/shard_map/add | solution.py:58
  25.4 0.2 fusion.17
  25.6 0.1 slice.179
  25.7 0.0 copy-start.3
  25.7 1.5 %fusion.4 = f32[3,3,64,512]{3,2,1,0:T(8,128)} fusion(f32[3,3,80,768]{3,2,1,0:T(8,128)S(1)} %bitcast.21, f32[2,3,64,512]{3,2,1,0:T(8,128)S(1)} %slice.179, f32[1,3,64,512]{3,2,1,0:T(8,128)S(1)} %fusion.17, f32[3,3,66,514]{3,2,1,0:T(8,128)S(1)} %fusion), kind=kLoop, calls=%fused_computation.10 | loop fusion | flops 1769472 | bytes 4718592 | tf_op jit(solution)/shard_map/add | solution.py:84
  27.2 0.0 copy-done.3
  27.2 0.7 copy.12.counts_ref
  27.8 56.7 %filter.1 = f32[18,64,512]{2,1,0:T(8,128)} custom-call(f32[9,64,512]{2,1,0:T(8,128)} %bitcast.23, s32[3,2]{1,0:T(4,128)} %copy.12.counts_ref, bf16[2048,256]{1,0:T(8,128)(2,1)} %constant.7.clone.txh_hbm, bf16[2048,256]{1,0:T(8,128)(2,1)} %constant.8.clone.txl_hbm, bf16[512,256]{1,0:T(8,128)(2,1)} %constant.9.clone.tzh_ref, ...), custom_call_target="tpu_custom_call" | custom-call | tf_op jit(solution)/shard_map/filter/pallas_call | solution.py:378
  84.5 3.4 %copy.14 = f32[6,3,64,512]{3,2,1,0:T(8,128)} copy(f32[6,3,64,512]{3,2,1,0:T(8,128)} %bitcast.22) | data formatting | bytes 4718592
Async XLA Ops:
  0.6 14.0 %copy-start.1 = (f32[3]{0:T(128)S(1)}, f32[3]{0:T(128)}, u32[]{:S(2)}) copy-start(f32[3]{0:T(128)} %param.11) | copy-start | bytes 40
  14.6 2.1 %copy-start = (f32[9,80,768]{2,1,0:T(8,128)S(1)}, f32[9,80,768]{2,1,0:T(8,128)}, u32[]{:S(2)}) copy-start(f32[9,80,768]{2,1,0:T(8,128)} %halo.1) | copy-start | bytes 6635524
  16.7 2.4 %copy-start.2 = (f32[3]{0:T(128)S(1)}, f32[3]{0:T(128)}, u32[]{:S(2)}) copy-start(f32[3]{0:T(128)} %param.12) | copy-start | bytes 40
  25.7 1.5 %copy-start.3 = (s32[3,2]{0,1:T(2,128)S(1)}, s32[3,2]{0,1:T(2,128)}, u32[]{:S(2)}) copy-start(s32[3,2]{0,1:T(2,128)} %param.13) | copy-start | bytes 76

commit v2 on v1

--- a/solution.py
+++ b/solution.py
@@ -49,47 +49,10 @@
     return one(a[0], b[0]) + (one(a[0], b[1]) + one(a[1], b[0]))
 
 
-def tendency_from(middle, east, west, north, south, slab, shear):
-    downflow = (east - west) * 0.5
-    crossflow = (north - south) * 0.5
-    diffusion = east + west + north + south - 4.0 * middle
-    holding = slab[:, None, None] + middle[0]
-    state = (
-        -holding[None] * downflow - middle[2][None] * crossflow + molecular_diffusivity * diffusion
-    )
-    return jnp.concatenate([state[0:1] - (shear[:, None, None] * middle[1])[None], state[1:]], axis=0)
-
-
-def rate(padded, slab, shear):
-    return tendency_from(
-        padded[:, :, 1:-1, 1:-1],
-        padded[:, :, 1:-1, 2:],
-        padded[:, :, 1:-1, :-2],
-        padded[:, :, 2:, 1:-1],
-        padded[:, :, :-2, 1:-1],
-        slab,
-        shear,
-    )
-
-
-def inner(cells, width):
-    return cells[:, :, width:-width, width:-width]
-
-
-def runge_kutta(padded, slab, shear):
-    first = inner(padded, 1) + time_step * rate(padded, slab, shear)
-    second = 0.75 * inner(padded, 2) + 0.25 * (
-        inner(first, 1) + time_step * rate(first, slab, shear)
-    )
-    return inner(padded, 3) / 3.0 + 2.0 / 3.0 * (
-        inner(second, 1) + time_step * rate(second, slab, shear)
-    )
-
-
-def halo_kernel(sizes, v_ref, out_ref, send_sem, recv_sem, local_sem):
+def halo_kernel(sizes, v_ref, zh_ref, xh_ref, corner_ref, strips, send_sem, recv_sem):
     gx_n, gz_n, grp_n = sizes
     z_n = gz_n * grp_n
-    _, cz, cx = v_ref.shape
+    count, cz, cx = v_ref.shape
     gx = lax.axis_index("gx")
     z = lax.axis_index("gz") * grp_n + lax.axis_index("grp")
     steps = [(dx, dz) for dx in (-1, 0, 1) for dz in (-1, 0, 1) if dx or dz]
@@ -105,45 +68,137 @@
     barrier = pltpu.get_barrier_semaphore()
     for dx, dz in steps:
         pl.semaphore_signal(barrier, inc=1, device_id=device(dx, dz), device_id_type=MESH)
+    for c in range(count):
+        strips[0, c] = v_ref[c, :, 0:LANES].T[0:ROWS]
+        strips[1, c] = v_ref[c, :, cx - LANES : cx].T[LANES - ROWS : LANES]
     pl.semaphore_wait(barrier, len(steps))
-    source_x = {1: pl.ds(cx - LANES, LANES), -1: pl.ds(0, LANES), 0: pl.ds(0, cx)}
-    target_x = {1: pl.ds(0, LANES), -1: pl.ds(LANES + cx, LANES), 0: pl.ds(LANES, cx)}
-    source_z = {1: pl.ds(cz - ROWS, ROWS), -1: pl.ds(0, ROWS), 0: pl.ds(0, cz)}
-    target_z = {1: pl.ds(0, ROWS), -1: pl.ds(ROWS + cz, ROWS), 0: pl.ds(ROWS, cz)}
+    edge_x = {1: pl.ds(cx - LANES, LANES), -1: pl.ds(0, LANES), 0: pl.ds(0, cx)}
+    edge_z = {1: pl.ds(cz - ROWS, ROWS), -1: pl.ds(0, ROWS)}
     copies = []
     for index, (dx, dz) in enumerate(steps):
-        copy = pltpu.make_async_remote_copy(
-            src_ref=v_ref.at[:, source_z[dz], source_x[dx]],
-            dst_ref=out_ref.at[:, target_z[dz], target_x[dx]],
-            send_sem=send_sem.at[index],
-            recv_sem=recv_sem.at[index],
-            device_id=device(dx, dz),
-            device_id_type=MESH,
+        side_x, side_z = int(dx > 0), int(dz > 0)
+        if dz == 0:
+            source, target = strips.at[side_x], xh_ref.at[side_x]
+        else:
+            source = v_ref.at[:, edge_z[dz], edge_x[dx]]
+            target = zh_ref.at[side_z] if dx == 0 else corner_ref.at[2 * side_z + side_x]
+        copies.append(
+            pltpu.make_async_remote_copy(
+                src_ref=source,
+                dst_ref=target,
+                send_sem=send_sem.at[index],
+                recv_sem=recv_sem.at[index],
+                device_id=device(dx, dz),
+                device_id_type=MESH,
+            )
         )
+    for copy in copies:
         copy.start()
-        copies.append(copy)
-    own = pltpu.make_async_copy(v_ref, out_ref.at[:, target_z[0], target_x[0]], local_sem)
-    own.start()
-    own.wait()
     for copy in copies:
         copy.wait()
 
 
-def with_halo(velocity, sizes):
+def halos(velocity, sizes):
     count, cz, cx = velocity.shape
+    vmem = pl.BlockSpec(memory_space=pltpu.VMEM)
     return pl.pallas_call(
         functools.partial(halo_kernel, sizes),
-        out_shape=jax.ShapeDtypeStruct((count, cz + 2 * ROWS, cx + 2 * LANES), f32),
-        in_specs=[pl.BlockSpec(memory_space=pltpu.VMEM)],
-        out_specs=pl.BlockSpec(memory_space=pl.ANY),
+        out_shape=(
+            jax.ShapeDtypeStruct((2, count, ROWS, cx), f32),
+            jax.ShapeDtypeStruct((2, count, ROWS, cz), f32),
+            jax.ShapeDtypeStruct((4, count, ROWS, LANES), f32),
+        ),
+        in_specs=[vmem],
+        out_specs=(vmem, vmem, vmem),
         scratch_shapes=[
+            pltpu.VMEM((2, count, ROWS, cz), f32),
             pltpu.SemaphoreType.DMA((8,)),
             pltpu.SemaphoreType.DMA((8,)),
-            pltpu.SemaphoreType.DMA,
         ],
         compiler_params=pltpu.CompilerParams(collective_id=0, has_side_effects=True),
         name="halo",
     )(velocity)
+
+
+def step_kernel(v_ref, zh_ref, xh_ref, corner_ref, slab_ref, shear_ref, out_ref, start, first, second):
+    p = pl.program_id(0)
+    slab, shear = slab_ref[p], shear_ref[p]
+    _, _, cz, cx = v_ref.shape
+    top = 2 * ROWS
+    lane = lax.broadcasted_iota(jnp.int32, (ROWS, LANES), 1)
+    width = cx + LANES
+    for c in range(3):
+        start[c, top : top + cz, 0:cx] = v_ref[c, 0]
+        strip = jnp.concatenate(
+            [xh_ref[0, c, 0], jnp.zeros((LANES - 2 * ROWS, cz), f32), xh_ref[1, c, 0]], axis=0
+        )
+        start[c, top : top + cz, cx:width] = strip.T
+        for side, row in ((1, top - ROWS), (0, top + cz)):
+            start[c, row : row + ROWS, 0:cx] = zh_ref[side, c, 0]
+            start[c, row : row + ROWS, cx:width] = jnp.where(
+                lane < LANES // 2, corner_ref[2 * side, c, 0], corner_ref[2 * side + 1, c, 0]
+            )
+
+    def block(source, row):
+        middle = [source[c, row : row + ROWS, :] for c in range(3)]
+        rates = []
+        for c in range(3):
+            north = source[c, row + 1 : row + 1 + ROWS, :]
+            south = source[c, row - 1 : row - 1 + ROWS, :]
+            east = pltpu.roll(middle[c], width - 1, 1)
+            west = pltpu.roll(middle[c], 1, 1)
+            value = (
+                -(slab + middle[0]) * ((east - west) * 0.5)
+                - middle[2] * ((north - south) * 0.5)
+                + molecular_diffusivity * (east + west + north + south - 4.0 * middle[c])
+            )
+            rates.append(value - shear * middle[1] if c == 0 else value)
+        return middle, rates
+
+    for row in range(ROWS, top + cz + ROWS, ROWS):
+        middle, rates = block(start, row)
+        for c in range(3):
+            first[c, row : row + ROWS, :] = middle[c] + time_step * rates[c]
+    for row in range(ROWS, top + cz + ROWS, ROWS):
+        middle, rates = block(first, row)
+        for c in range(3):
+            second[c, row : row + ROWS, :] = 0.75 * start[c, row : row + ROWS, :] + 0.25 * (
+                middle[c] + time_step * rates[c]
+            )
+    for row in range(top, top + cz, ROWS):
+        middle, rates = block(second, row)
+        for c in range(3):
+            value = start[c, row : row + ROWS, :] * (1.0 / 3.0) + (2.0 / 3.0) * (
+                middle[c] + time_step * rates[c]
+            )
+            out_ref[c, 0, row - top : row - top + ROWS, :] = value[:, 0:cx]
+
+
+def advance(velocity, slab, shear, sizes):
+    three, planes, cz, cx = velocity.shape
+    zh, xh, corner = halos(velocity.reshape(three * planes, cz, cx), sizes)
+    smem = pl.BlockSpec(memory_space=pltpu.SMEM)
+    main = pl.BlockSpec((3, 1, cz, cx), lambda p: (0, p, 0, 0))
+
+    def edge(sides, lanes):
+        return pl.BlockSpec((sides, 3, 1, ROWS, lanes), lambda p: (0, 0, p, 0, 0))
+
+    return pl.pallas_call(
+        step_kernel,
+        grid=(planes,),
+        out_shape=jax.ShapeDtypeStruct(velocity.shape, f32),
+        in_specs=[main, edge(2, cx), edge(2, cz), edge(4, LANES), smem, smem],
+        out_specs=main,
+        scratch_shapes=[pltpu.VMEM((3, cz + 4 * ROWS, cx + LANES), f32)] * 3,
+        name="step",
+    )(
+        velocity,
+        zh.reshape(2, three, planes, ROWS, cx),
+        xh.reshape(2, three, planes, ROWS, cz),
+        corner.reshape(4, three, planes, ROWS, LANES),
+        slab,
+        shear,
+    )
 
 
 def filter_kernel(
@@ -413,10 +468,7 @@
 
 def local(sizes, velocity, slab, shear, mode_counts):
     three, planes, cz, cx = velocity.shape
-    padded = with_halo(velocity.reshape(three * planes, cz, cx), sizes)
-    padded = padded.reshape(three, planes, cz + 2 * ROWS, cx + 2 * LANES)
-    padded = padded[:, :, ROWS - 3 : ROWS + cz + 3, LANES - 3 : LANES + cx + 3]
-    advanced = runge_kutta(padded, slab, shear)
+    advanced = advance(velocity, slab, shear, sizes)
     stress = filtered_stress(advanced.reshape(three * planes, cz, cx), mode_counts, sizes)
     return advanced, stress.reshape(6, planes, cz, cx)
 

time: 88.1 us -> 84.6 us (0.960)
  other arithmetic: 12 us -> 0 us
  Pallas kernels: 70.7 us -> 78.9 us
    add x6 -> x0, other arithmetic: 8.83 us -> none  [the longest x3 5.54 us: tendency_from(): -holding[None] * downflow - middle[2][None] * crossflow]
    pallas_call x1 -> x2, Pallas kernels: 14 us -> 22.2 us  [the longest x1 14.7 us: halos(): pl.pallas_call(functools.partial(halo_kernel, sizes), out_shape=(jax.Shap...]
    mul x3 -> x0, other arithmetic: 2.58 us -> none  [tendency_from(): -holding[None] * downflow - middle[2][None] * crossflow]
    unnamed x10 -> x2, local copies, waits for them, and re-layouts: 4.2 us -> 4.71 us
where the time goes in v2:
time: 84.6 us; the launch traced here: 84.3 us
  Pallas kernels  78.9 us (93%)
  local copies, waits for them, and re-layouts  4.71 us (6%)
    pallas_call x1, Pallas kernels, filtered_stress(): pl.pallas_call(functools.partial(filter_kernel, sizes, planes), out_shape...  56.7 us
    pallas_call x1, Pallas kernels, halos(): pl.pallas_call(functools.partial(halo_kernel, sizes), out_shape=(jax.Shap...  14.7 us
    pallas_call x1, Pallas kernels, advance(): pl.pallas_call(step_kernel, grid=(planes,), out_shape=jax.ShapeDtypeStruc...  7.59 us
    unnamed x2, local copies, waits for them, and re-layouts  4.71 us

profile of v2, /device:TPU:31, one launch (start us, length us, event | category | flops | bytes accessed | tf_op | source)
XLA Modules:
  0.0 84.3 jit_solution(6531324645031321058)
XLA Ops:
  0.6 1.3 %copy.12.counts_ref = s32[3,2]{1,0:T(4,128)} copy(s32[3,2]{0,1:T(2,128)} %param.13) | data formatting | bytes 48 | tf_op args[3]
  2.0 14.7 %halo.1 = (f32[2,9,8,512]{3,2,1,0:T(8,128)}, f32[2,9,8,64]{3,2,1,0:T(8,128)}, f32[4,9,8,128]{3,2,1,0:T(8,128)}) custom-call(f32[9,64,512]{2,1,0:T(8,128)} %bitcast.7), custom_call_target="tpu_custom_call" | custom-call | tf_op jit(solution)/shard_map/halo/pallas_call | solution.py:104
  16.6 7.6 %step.1 = f32[3,3,64,512]{3,2,1,0:T(8,128)} custom-call(f32[3,3,64,512]{3,2,1,0:T(8,128)} %v_ref.1, f32[2,3,3,8,512]{4,3,2,1,0:T(8,128)} %bitcast.9, f32[2,3,3,8,64]{4,3,2,1,0:T(8,128)} %bitcast.11, f32[4,3,3,8,128]{4,3,2,1,0:T(8,128)} %bitcast.10, f32[3]{0:T(128)} %slab_ref.1, f32[3]{0:T(128)} %shear_ref.1), custom_call_target="tpu_custom_call" | custom-call | tf_op jit(solution)/shard_map/step/pallas_call | solution.py:186
  24.2 56.7 %filter.1 = f32[18,64,512]{2,1,0:T(8,128)} custom-call(f32[9,64,512]{2,1,0:T(8,128)} %bitcast.8, s32[3,2]{1,0:T(4,128)} %copy.12.counts_ref, bf16[2048,256]{1,0:T(8,128)(2,1)} %constant.12.clone.txh_hbm, bf16[2048,256]{1,0:T(8,128)(2,1)} %constant.13.clone.txl_hbm, bf16[512,256]{1,0:T(8,128)(2,1)} %constant.14.clone.tzh_ref, ...), custom_call_target="tpu_custom_call" | custom-call | tf_op jit(solution)/shard_map/filter/pallas_call | solution.py:433
  80.9 3.4 %copy.14 = f32[6,3,64,512]{3,2,1,0:T(8,128)} copy(f32[6,3,64,512]{3,2,1,0:T(8,128)} %bitcast.6) | data formatting | bytes 4718592

commit v3 on v2

--- a/solution.py
+++ b/solution.py
@@ -202,14 +202,15 @@
 
 
 def filter_kernel(
-    sizes, planes, adv_ref, counts_ref, txh_hbm, txl_hbm, tzh_ref, tzl_ref, tth_ref, ttl_ref, out_ref,
-    high, low, txh, txl, part_send, part_keep, part_recv, y_send, y_recv, z_send, z_recv, z_out, gath,
+    sizes, planes, adv_ref, counts_ref, txh_hbm, txl_hbm, tzh_ref, tzl_ref, tth_ref, ttl_ref, gath,
+    high, low, txh, txl, part_send, part_keep, part_recv, y_send, y_recv, z_send, z_recv, z_out,
     table_sem, ps_sem, pr_sem, ys_sem, yr_sem, zs_sem, zr_sem, os_sem, gr_sem, gy_sem, gp_sem,
 ):
     gx_n, gz_n, grp_n = sizes
     z_n = gz_n * grp_n
     y_n = gx_n // 2
-    units = gath.shape[0] // gx_n
+    chunks, total_units, _, lanes = gath.shape
+    units = total_units // gx_n
     _, cz, cx = adv_ref.shape
     gx = lax.axis_index("gx")
     z = lax.axis_index("gz") * grp_n + lax.axis_index("grp")
@@ -257,160 +258,207 @@
         return carry
 
     lax.fori_loop(0, planes, prepare, 0)
-    for unit in range(planes * FIELDS, gath.shape[0]):
+    for unit in range(planes * FIELDS, total_units):
         high[unit] = jnp.zeros((cz, cx), bf16)
         low[unit] = jnp.zeros((cz, cx), bf16)
     for copy in tables:
         copy.wait()
-    pl.semaphore_wait(barrier, len(friends))
-
-    def analyse(block):
+
+    def analyse(block, target, d):
         chosen = pl.ds(block * units, units)
         rows = (high[chosen].reshape(units * cz, cx), low[chosen].reshape(units * cz, cx))
-        return dot3(rows, (txh[...], txl[...])).reshape(units, cz, MODES)
+        sums = dot3(rows, (txh[...], txl[...]))
+        for h in range(chunks):
+            target[h, d] = sums[:, h * lanes : (h + 1) * lanes].reshape(units, cz, lanes)
+
+    def to_partner(h, d):
+        return remote(
+            part_send.at[h, d], part_recv.at[h, d], ps_sem.at[h, d], pr_sem.at[h, d], at_x(y, other)
+        )
+
+    def to_y(h, d):
+        return remote(
+            y_send.at[h, d - 1], y_recv.at[h, d - 1], ys_sem.at[h, d - 1], yr_sem.at[h, d - 1],
+            at_x(lax.rem(y + d, y_n), core),
+        )
+
+    def send_y(h, d):
+        to_partner(h, d).wait_recv()
+        y_send[h, d - 1] = part_keep[h, d] + part_recv[h, d]
+        to_y(h, d).start()
+
+    def forward(h, k):
+        return remote(z_send.at[h, k], z_recv.at[h, z], zs_sem.at[h, k], zr_sem.at[h, z], at_z(k))
+
+    unit = gx * units + z
+
+    def back(h, s, slot):
+        return remote(z_out.at[h, s], gath.at[h, slot], os_sem.at[h, s], gr_sem.at[h, slot], at_z(s))
+
+    def send_z(h):
+        to_partner(h, 0).wait_recv()
+        for d in range(1, y_n):
+            to_y(h, d).wait_recv()
+        for k in range(units):
+            total = part_keep[h, 0, k] + part_recv[h, 0, k]
+            for d in range(1, y_n):
+                total = total + y_recv[h, d - 1, k]
+            z_send[h, k] = total
+
+            @pl.when(z != k)
+            def _():
+                forward(h, k).start()
+
+            @pl.when(z == k)
+            def _():
+                z_recv[h, z] = total
+
+    def filter_lines(h):
+        for s in range(z_n):
+
+            @pl.when(z != s)
+            def _():
+                remote(
+                    z_send.at[h, 0], z_recv.at[h, s], zs_sem.at[h, 0], zr_sem.at[h, s], at_z(s)
+                ).wait_recv()
+
+        plane = jnp.minimum(lax.div(unit, FIELDS), planes - 1)
+        limit_x, limit_z = counts_ref[plane, 0], counts_ref[plane, 1]
+
+        def numbers(axis, start):
+            column = lax.broadcasted_iota(jnp.int32, (MODES, lanes), axis) + start
+            half = MODES // 2
+            return jnp.where(column < half, column, column - half + 1), column
+
+        def weights(column, length):
+            return jnp.where(column == 0, f32(1.0 / length), f32(2.0 / length))
+
+        kz, nz = numbers(0, 0)
+        kx, nx = numbers(1, h * lanes)
+        scale = weights(nz, z_n * cz) * weights(nx, gx_n * cx)
+        scale = jnp.where((kz <= limit_z) & (kx <= limit_x), scale, 0.0)
+        lines = split(z_recv[h].reshape(z_n * cz, lanes))
+        spectral = dot3((tth_ref[...], ttl_ref[...]), lines) * scale
+        z_out[h] = dot3((tzh_ref[...], tzl_ref[...]), split(spectral)).reshape(z_n, cz, lanes)
+        for s in range(z_n):
+
+            @pl.when(z != s)
+            def _():
+                back(h, s, unit).start()
+
+            @pl.when(z == s)
+            def _():
+                gath[h, unit] = z_out[h, s]
+
+    def spread(h, slot, k, d):
+        return remote(
+            gath.at[h, slot], gath.at[h, slot], gy_sem.at[h, d - 1, k], gr_sem.at[h, slot],
+            at_x(lax.rem(y + d, y_n), core),
+        )
+
+    def share(h, slot, d, k):
+        return remote(
+            gath.at[h, slot], gath.at[h, slot], gp_sem.at[h, d, k], gr_sem.at[h, slot], at_x(y, other)
+        )
+
+    def spread_own(h):
+        for k in range(units):
+            slot = gx * units + k
+
+            @pl.when(z != k)
+            def _():
+                back(h, 0, slot).wait_recv()
+
+            for d in range(1, y_n):
+                spread(h, slot, k, d).start()
+            share(h, slot, 0, k).start()
+
+    def share_others(h):
+        for d in range(1, y_n):
+            for k in range(units):
+                slot = (2 * lax.rem(y + d, y_n) + core) * units + k
+                back(h, 0, slot).wait_recv()
+                share(h, slot, d, k).start()
 
     order = list(range(1, y_n)) + [0]
-    to_partner = [
-        remote(part_send.at[d], part_recv.at[d], ps_sem.at[d], pr_sem.at[d], at_x(y, other))
-        for d in range(y_n)
-    ]
+    first = True
     for d in order:
-        part_send[d] = analyse(2 * lax.rem(y + d, y_n) + other)
-        to_partner[d].start()
-    for d in order:
-        part_keep[d] = analyse(2 * lax.rem(y + d, y_n) + core)
-    to_y = {
-        d: remote(
-            y_send.at[d - 1], y_recv.at[d - 1], ys_sem.at[d - 1], yr_sem.at[d - 1],
-            at_x(lax.rem(y + d, y_n), core),
-        )
-        for d in range(1, y_n)
-    }
-    for d in range(1, y_n):
-        to_partner[d].wait_recv()
-        y_send[d - 1] = part_keep[d] + part_recv[d]
-        to_y[d].start()
-    to_partner[0].wait_recv()
-    for d in range(1, y_n):
-        to_y[d].wait_recv()
-
-    def forward(k, device_slot):
-        return remote(z_send.at[k], z_recv.at[z], zs_sem.at[k], zr_sem.at[device_slot], at_z(k))
-
-    for k in range(units):
-        total = part_keep[0, k] + part_recv[0, k]
-        for d in range(1, y_n):
-            total = total + y_recv[d - 1, k]
-        z_send[k] = total
-
-        @pl.when(z != k)
-        def _():
-            forward(k, z).start()
-
-        @pl.when(z == k)
-        def _():
-            z_recv[z] = total
-
-    unit = gx * units + z
-
-    def back(s, slot):
-        return remote(z_out.at[s], gath.at[slot], os_sem.at[s], gr_sem.at[slot], at_z(s))
+        analyse(2 * lax.rem(y + d, y_n) + other, part_send, d)
+        if first:
+            pl.semaphore_wait(barrier, len(friends))
+            first = False
+        for h in range(chunks):
+            to_partner(h, d).start()
+        analyse(2 * lax.rem(y + d, y_n) + core, part_keep, d)
+        if d:
+            for h in range(chunks):
+                send_y(h, d)
+    for h in range(chunks):
+        send_z(h)
 
     @pl.when(z < units)
     def _():
-        for s in range(z_n):
-
-            @pl.when(z != s)
-            def _():
-                remote(z_send.at[0], z_recv.at[s], zs_sem.at[0], zr_sem.at[s], at_z(s)).wait_recv()
-
-        plane = jnp.minimum(lax.div(unit, FIELDS), planes - 1)
-        limit_x, limit_z = counts_ref[plane, 0], counts_ref[plane, 1]
-
-        def numbers(axis):
-            column = lax.broadcasted_iota(jnp.int32, (MODES, MODES), axis)
-            half = MODES // 2
-            return jnp.where(column < half, column, column - half + 1), column
-
-        def weights(column, length):
-            return jnp.where(column == 0, f32(1.0 / length), f32(2.0 / length))
-
-        kz, nz = numbers(0)
-        kx, nx = numbers(1)
-        scale = weights(nz, z_n * cz) * weights(nx, gx_n * cx)
-        scale = jnp.where((kz <= limit_z) & (kx <= limit_x), scale, 0.0)
-        lines = split(z_recv[...].reshape(z_n * cz, MODES))
-        spectral = dot3((tth_ref[...], ttl_ref[...]), lines) * scale
-        z_out[...] = dot3((tzh_ref[...], tzl_ref[...]), split(spectral)).reshape(z_n, cz, MODES)
-        for s in range(z_n):
-
-            @pl.when(z != s)
-            def _():
-                back(s, unit).start()
-
-            @pl.when(z == s)
-            def _():
-                gath[unit] = z_out[s]
-
-    def spread(slot, k, d):
-        return remote(
-            gath.at[slot], gath.at[slot], gy_sem.at[d - 1, k], gr_sem.at[slot],
-            at_x(lax.rem(y + d, y_n), core),
-        )
-
-    def share(slot, d, k):
-        return remote(gath.at[slot], gath.at[slot], gp_sem.at[d, k], gr_sem.at[slot], at_x(y, other))
-
-    for k in range(units):
-        slot = gx * units + k
-
-        @pl.when(z != k)
+        filter_lines(0)
+
+    for h in range(chunks):
+        spread_own(h)
+        if h + 1 < chunks:
+
+            @pl.when(z < units)
+            def _():
+                filter_lines(h + 1)
+
+        share_others(h)
+    for h in range(chunks):
+        for d in range(y_n):
+            for k in range(units):
+                back(h, 0, (2 * lax.rem(y + d, y_n) + other) * units + k).wait_recv()
+
+    for h in range(chunks):
+        for d in range(y_n):
+            to_partner(h, d).wait_send()
+        for d in range(1, y_n):
+            to_y(h, d).wait_send()
+        for k in range(units):
+
+            @pl.when(z != k)
+            def _():
+                forward(h, k).wait_send()
+
+            for d in range(1, y_n):
+                spread(h, gx * units + k, k, d).wait_send()
+            for d in range(y_n):
+                share(h, gx * units + k, d, k).wait_send()
+
+        @pl.when(z < units)
         def _():
-            back(0, slot).wait_recv()
-
-        for d in range(1, y_n):
-            spread(slot, k, d).start()
-        share(slot, 0, k).start()
-    for d in range(1, y_n):
-        for k in range(units):
-            slot = (2 * lax.rem(y + d, y_n) + core) * units + k
-            back(0, slot).wait_recv()
-            share(slot, d, k).start()
-    for d in range(y_n):
-        for k in range(units):
-            back(0, (2 * lax.rem(y + d, y_n) + other) * units + k).wait_recv()
-
-    def synthesise(p, carry):
-        rows = split(gath[pl.ds(p * FIELDS, FIELDS)].reshape(FIELDS * cz, MODES))
-        filtered = dot3(rows, (txh[...], txl[...]), ((1,), (1,))).reshape(FIELDS, cz, cx)
-        for q, (a, b) in enumerate(zip(pair_first, pair_second)):
-            out_ref[q * planes + p] = filtered[3 + q] - filtered[a] * filtered[b]
-        return carry
-
-    lax.fori_loop(0, planes, synthesise, 0)
-
-    for d in range(y_n):
-        to_partner[d].wait_send()
-    for d in range(1, y_n):
-        to_y[d].wait_send()
-    for k in range(units):
-
-        @pl.when(z != k)
-        def _():
-            forward(k, z).wait_send()
-
-        for d in range(1, y_n):
-            spread(gx * units + k, k, d).wait_send()
-        for d in range(y_n):
-            share(gx * units + k, d, k).wait_send()
-
-    @pl.when(z < units)
+            for s in range(z_n):
+
+                @pl.when(z != s)
+                def _():
+                    back(h, s, unit).wait_send()
+
+
+def synthesis_kernel(gath_ref, txh_hbm, txl_hbm, out_ref, txh, txl, table_sem):
+    chunks, _, cz, _ = gath_ref.shape
+    cx = txh.shape[0]
+
+    @pl.when(pl.program_id(0) == 0)
     def _():
-        for s in range(z_n):
-
-            @pl.when(z != s)
-            def _():
-                back(s, unit).wait_send()
+        mine = pl.ds(pl.multiple_of(lax.axis_index("gx") * cx, cx), cx)
+        copies = [
+            pltpu.make_async_copy(txh_hbm.at[mine, :], txh, table_sem.at[0]),
+            pltpu.make_async_copy(txl_hbm.at[mine, :], txl, table_sem.at[1]),
+        ]
+        for copy in copies:
+            copy.start()
+        for copy in copies:
+            copy.wait()
+
+    rows = jnp.concatenate([gath_ref[h].reshape(FIELDS * cz, -1) for h in range(chunks)], axis=1)
+    filtered = dot3(split(rows), (txh[...], txl[...]), ((1,), (1,))).reshape(FIELDS, cz, cx)
+    for q, (a, b) in enumerate(zip(pair_first, pair_second)):
+        out_ref[q, 0] = filtered[3 + q] - filtered[a] * filtered[b]
 
 
 def filtered_stress(advanced, mode_counts, sizes):
@@ -421,7 +469,7 @@
     planes = count // 3
     units = -(-FIELDS * planes // gx_n)
     assert gx_n % 2 == 0 and units <= z_n
-    txh, txl = split_table(wave_table(cx * gx_n))
+    txh, txl = (jnp.asarray(t) for t in split_table(wave_table(cx * gx_n)))
     table_z = wave_table(cz * z_n)
     tzh, tzl = split_table(table_z)
     tth, ttl = split_table(table_z.T)
@@ -430,9 +478,11 @@
     anywhere = pl.BlockSpec(memory_space=pl.ANY)
     others = max(y_n - 1, 1)
     total = gx_n * units
-    return pl.pallas_call(
+    chunks = 2
+    lanes = MODES // chunks
+    gathered = pl.pallas_call(
         functools.partial(filter_kernel, sizes, planes),
-        out_shape=jax.ShapeDtypeStruct((6 * planes, cz, cx), f32),
+        out_shape=jax.ShapeDtypeStruct((chunks, total, cz, lanes), f32),
         in_specs=[vmem, pl.BlockSpec(memory_space=pltpu.SMEM), anywhere, anywhere, vmem, vmem, vmem, vmem],
         out_specs=vmem,
         scratch_shapes=[
@@ -440,37 +490,47 @@
             pltpu.VMEM((total, cz, cx), bf16),
             pltpu.VMEM((cx, MODES), bf16),
             pltpu.VMEM((cx, MODES), bf16),
-            pltpu.VMEM((y_n, units, cz, MODES), f32),
-            pltpu.VMEM((y_n, units, cz, MODES), f32),
-            pltpu.VMEM((y_n, units, cz, MODES), f32),
-            pltpu.VMEM((others, units, cz, MODES), f32),
-            pltpu.VMEM((others, units, cz, MODES), f32),
-            pltpu.VMEM((units, cz, MODES), f32),
-            pltpu.VMEM((z_n, cz, MODES), f32),
-            pltpu.VMEM((z_n, cz, MODES), f32),
-            pltpu.VMEM((total, cz, MODES), f32),
+            pltpu.VMEM((chunks, y_n, units, cz, lanes), f32),
+            pltpu.VMEM((chunks, y_n, units, cz, lanes), f32),
+            pltpu.VMEM((chunks, y_n, units, cz, lanes), f32),
+            pltpu.VMEM((chunks, others, units, cz, lanes), f32),
+            pltpu.VMEM((chunks, others, units, cz, lanes), f32),
+            pltpu.VMEM((chunks, units, cz, lanes), f32),
+            pltpu.VMEM((chunks, z_n, cz, lanes), f32),
+            pltpu.VMEM((chunks, z_n, cz, lanes), f32),
             dma((2,)),
-            dma((y_n,)),
-            dma((y_n,)),
-            dma((others,)),
-            dma((others,)),
-            dma((units,)),
-            dma((z_n,)),
-            dma((z_n,)),
-            dma((total,)),
-            dma((others, units)),
-            dma((y_n, units)),
+            dma((chunks, y_n)),
+            dma((chunks, y_n)),
+            dma((chunks, others)),
+            dma((chunks, others)),
+            dma((chunks, units)),
+            dma((chunks, z_n)),
+            dma((chunks, z_n)),
+            dma((chunks, total)),
+            dma((chunks, others, units)),
+            dma((chunks, y_n, units)),
         ],
         compiler_params=pltpu.CompilerParams(collective_id=1, has_side_effects=True),
         name="filter",
-    )(advanced, mode_counts, *(jnp.asarray(t) for t in (txh, txl, tzh, tzl, tth, ttl)))
+    )(advanced, mode_counts, txh, txl, *(jnp.asarray(t) for t in (tzh, tzl, tth, ttl)))
+    return pl.pallas_call(
+        synthesis_kernel,
+        grid=(planes,),
+        out_shape=jax.ShapeDtypeStruct((6, planes, cz, cx), f32),
+        in_specs=[
+            pl.BlockSpec((chunks, FIELDS, cz, lanes), lambda p: (0, p, 0, 0)), anywhere, anywhere
+        ],
+        out_specs=pl.BlockSpec((6, 1, cz, cx), lambda p: (0, p, 0, 0)),
+        scratch_shapes=[pltpu.VMEM((cx, MODES), bf16), pltpu.VMEM((cx, MODES), bf16), dma((2,))],
+        name="synthesis",
+    )(gathered, txh, txl)
 
 
 def local(sizes, velocity, slab, shear, mode_counts):
     three, planes, cz, cx = velocity.shape
     advanced = advance(velocity, slab, shear, sizes)
     stress = filtered_stress(advanced.reshape(three * planes, cz, cx), mode_counts, sizes)
-    return advanced, stress.reshape(6, planes, cz, cx)
+    return advanced, stress
 
 
 def solution(mesh):

time: 84.6 us -> 79.4 us (0.939)
  the two profiles are of different devices: /device:TPU:31 before, /device:TPU:0 now
where the time goes in v3:
time: 79.4 us; the launch traced here: 79 us
  Pallas kernels  77 us (97%)
  local copies, waits for them, and re-layouts  1.34 us (2%)
    pallas_call x1, Pallas kernels, filtered_stress(): pl.pallas_call(functools.partial(filter_kernel, sizes, planes), out_shape...  46.2 us
    pallas_call x1, Pallas kernels, halos(): pl.pallas_call(functools.partial(halo_kernel, sizes), out_shape=(jax.Shap...  17.5 us
    pallas_call x1, Pallas kernels, advance(): pl.pallas_call(step_kernel, grid=(planes,), out_shape=jax.ShapeDtypeStruc...  7.59 us
    pallas_call x1, Pallas kernels, filtered_stress(): pl.pallas_call(synthesis_kernel, grid=(planes,), out_shape=jax.ShapeDtype...  5.75 us

profile of v3, /device:TPU:0, one launch (start us, length us, event | category | flops | bytes accessed | tf_op | source)
XLA Modules:
  0.0 79.0 jit_solution(2338786551124360881)
XLA Ops:
  0.6 1.3 %copy.12.counts_ref = s32[3,2]{1,0:T(4,128)} copy(s32[3,2]{0,1:T(2,128)} %param.13) | data formatting | bytes 48 | tf_op args[3]
  2.0 17.5 %halo.1 = (f32[2,9,8,512]{3,2,1,0:T(8,128)}, f32[2,9,8,64]{3,2,1,0:T(8,128)}, f32[4,9,8,128]{3,2,1,0:T(8,128)}) custom-call(f32[9,64,512]{2,1,0:T(8,128)} %bitcast.5), custom_call_target="tpu_custom_call" | custom-call | tf_op jit(solution)/shard_map/halo/pallas_call | solution.py:104
  19.5 7.6 %step.1 = f32[3,3,64,512]{3,2,1,0:T(8,128)} custom-call(f32[3,3,64,512]{3,2,1,0:T(8,128)} %v_ref.1, f32[2,3,3,8,512]{4,3,2,1,0:T(8,128)} %bitcast.7, f32[2,3,3,8,64]{4,3,2,1,0:T(8,128)} %bitcast.9, f32[4,3,3,8,128]{4,3,2,1,0:T(8,128)} %bitcast.8, f32[3]{0:T(128)} %slab_ref.1, f32[3]{0:T(128)} %shear_ref.1), custom_call_target="tpu_custom_call" | custom-call | tf_op jit(solution)/shard_map/step/pallas_call | solution.py:186
  27.1 46.2 %filter.1.gath_ref = f32[2,28,64,128]{3,2,1,0:T(8,128)} custom-call(f32[9,64,512]{2,1,0:T(8,128)} %bitcast.6, s32[3,2]{1,0:T(4,128)} %copy.12.counts_ref, bf16[2048,256]{1,0:T(8,128)(2,1)} %constant.12.clone.txh_hbm, bf16[2048,256]{1,0:T(8,128)(2,1)} %constant.13.clone.txl_hbm, bf16[512,256]{1,0:T(8,128)(2,1)} %constant.14.clone.tzh_ref, ...), custom_call_target="tpu_custom_call" | custom-call | tf_op jit(solution)/shard_map/filter/pallas_call | solution.py:483
  73.3 5.7 %synthesis.1 = f32[6,3,64,512]{3,2,1,0:T(8,128)} custom-call(f32[2,28,64,128]{3,2,1,0:T(8,128)} %filter.1.gath_ref, bf16[2048,256]{1,0:T(8,128)(2,1)} %constant.12.clone.txh_hbm, bf16[2048,256]{1,0:T(8,128)(2,1)} %constant.13.clone.txl_hbm), custom_call_target="tpu_custom_call" | custom-call | tf_op jit(solution)/shard_map/synthesis/pallas_call | solution.py:516

commit v4 on v3

--- a/solution.py
+++ b/solution.py
@@ -276,16 +276,19 @@
             part_send.at[h, d], part_recv.at[h, d], ps_sem.at[h, d], pr_sem.at[h, d], at_x(y, other)
         )
 
-    def to_y(h, d):
+    def to_y(h, d, k):
         return remote(
-            y_send.at[h, d - 1], y_recv.at[h, d - 1], ys_sem.at[h, d - 1], yr_sem.at[h, d - 1],
+            y_send.at[h, d - 1, k], y_recv.at[h, d - 1, k], ys_sem.at[h, d - 1, k], yr_sem.at[h, d - 1, k],
             at_x(lax.rem(y + d, y_n), core),
         )
+
+    turns = [lax.rem(z + i, units) for i in range(units)]
 
     def send_y(h, d):
         to_partner(h, d).wait_recv()
-        y_send[h, d - 1] = part_keep[h, d] + part_recv[h, d]
-        to_y(h, d).start()
+        for k in turns:
+            y_send[h, d - 1, k] = part_keep[h, d, k] + part_recv[h, d, k]
+            to_y(h, d, k).start()
 
     def forward(h, k):
         return remote(z_send.at[h, k], z_recv.at[h, z], zs_sem.at[h, k], zr_sem.at[h, z], at_z(k))
@@ -297,9 +300,9 @@
 
     def send_z(h):
         to_partner(h, 0).wait_recv()
-        for d in range(1, y_n):
-            to_y(h, d).wait_recv()
-        for k in range(units):
+        for k in turns:
+            for d in range(1, y_n):
+                to_y(h, d, k).wait_recv()
             total = part_keep[h, 0, k] + part_recv[h, 0, k]
             for d in range(1, y_n):
                 total = total + y_recv[h, d - 1, k]
@@ -393,13 +396,14 @@
         if d:
             for h in range(chunks):
                 send_y(h, d)
-    for h in range(chunks):
-        send_z(h)
+    send_z(0)
 
     @pl.when(z < units)
     def _():
         filter_lines(0)
 
+    for h in range(1, chunks):
+        send_z(h)
     for h in range(chunks):
         spread_own(h)
         if h + 1 < chunks:
@@ -418,7 +422,8 @@
         for d in range(y_n):
             to_partner(h, d).wait_send()
         for d in range(1, y_n):
-            to_y(h, d).wait_send()
+            for k in range(units):
+                to_y(h, d, k).wait_send()
         for k in range(units):
 
             @pl.when(z != k)
@@ -501,8 +506,8 @@
             dma((2,)),
             dma((chunks, y_n)),
             dma((chunks, y_n)),
-            dma((chunks, others)),
-            dma((chunks, others)),
+            dma((chunks, others, units)),
+            dma((chunks, others, units)),
             dma((chunks, units)),
             dma((chunks, z_n)),
             dma((chunks, z_n)),

time: 79.4 us -> 79.1 us (level)
  no operation moved by 1% of the time
where the time goes in v4:
time: 79.1 us; the launch traced here: 78.6 us
  Pallas kernels  76.6 us (97%)
  local copies, waits for them, and re-layouts  1.34 us (2%)
    pallas_call x1, Pallas kernels, filtered_stress(): pl.pallas_call(functools.partial(filter_kernel, sizes, planes), out_shape...  45.7 us
    pallas_call x1, Pallas kernels, halos(): pl.pallas_call(functools.partial(halo_kernel, sizes), out_shape=(jax.Shap...  17.5 us
    pallas_call x1, Pallas kernels, advance(): pl.pallas_call(step_kernel, grid=(planes,), out_shape=jax.ShapeDtypeStruc...  7.59 us
    pallas_call x1, Pallas kernels, filtered_stress(): pl.pallas_call(synthesis_kernel, grid=(planes,), out_shape=jax.ShapeDtype...  5.75 us

profile of v4, /device:TPU:0, one launch (start us, length us, event | category | flops | bytes accessed | tf_op | source)
XLA Modules:
  0.0 78.6 jit_solution(2998920138020072680)
XLA Ops:
  0.6 1.3 %copy.12.counts_ref = s32[3,2]{1,0:T(4,128)} copy(s32[3,2]{0,1:T(2,128)} %param.13) | data formatting | bytes 48 | tf_op args[3]
  2.0 17.5 %halo.1 = (f32[2,9,8,512]{3,2,1,0:T(8,128)}, f32[2,9,8,64]{3,2,1,0:T(8,128)}, f32[4,9,8,128]{3,2,1,0:T(8,128)}) custom-call(f32[9,64,512]{2,1,0:T(8,128)} %bitcast.5), custom_call_target="tpu_custom_call" | custom-call | tf_op jit(solution)/shard_map/halo/pallas_call | solution.py:104
  19.5 7.6 %step.1 = f32[3,3,64,512]{3,2,1,0:T(8,128)} custom-call(f32[3,3,64,512]{3,2,1,0:T(8,128)} %v_ref.1, f32[2,3,3,8,512]{4,3,2,1,0:T(8,128)} %bitcast.7, f32[2,3,3,8,64]{4,3,2,1,0:T(8,128)} %bitcast.9, f32[4,3,3,8,128]{4,3,2,1,0:T(8,128)} %bitcast.8, f32[3]{0:T(128)} %slab_ref.1, f32[3]{0:T(128)} %shear_ref.1), custom_call_target="tpu_custom_call" | custom-call | tf_op jit(solution)/shard_map/step/pallas_call | solution.py:186
  27.1 45.7 %filter.1.gath_ref = f32[2,28,64,128]{3,2,1,0:T(8,128)} custom-call(f32[9,64,512]{2,1,0:T(8,128)} %bitcast.6, s32[3,2]{1,0:T(4,128)} %copy.12.counts_ref, bf16[2048,256]{1,0:T(8,128)(2,1)} %constant.12.clone.txh_hbm, bf16[2048,256]{1,0:T(8,128)(2,1)} %constant.13.clone.txl_hbm, bf16[512,256]{1,0:T(8,128)(2,1)} %constant.14.clone.tzh_ref, ...), custom_call_target="tpu_custom_call" | custom-call | tf_op jit(solution)/shard_map/filter/pallas_call | solution.py:488
  72.8 5.7 %synthesis.1 = f32[6,3,64,512]{3,2,1,0:T(8,128)} custom-call(f32[2,28,64,128]{3,2,1,0:T(8,128)} %filter.1.gath_ref, bf16[2048,256]{1,0:T(8,128)(2,1)} %constant.12.clone.txh_hbm, bf16[2048,256]{1,0:T(8,128)(2,1)} %constant.13.clone.txl_hbm), custom_call_target="tpu_custom_call" | custom-call | tf_op jit(solution)/shard_map/synthesis/pallas_call | solution.py:521

commit v5 on v4

--- a/solution.py
+++ b/solution.py
@@ -49,94 +49,27 @@
     return one(a[0], b[0]) + (one(a[0], b[1]) + one(a[1], b[0]))
 
 
-def halo_kernel(sizes, v_ref, zh_ref, xh_ref, corner_ref, strips, send_sem, recv_sem):
-    gx_n, gz_n, grp_n = sizes
-    z_n = gz_n * grp_n
-    count, cz, cx = v_ref.shape
-    gx = lax.axis_index("gx")
-    z = lax.axis_index("gz") * grp_n + lax.axis_index("grp")
-    steps = [(dx, dz) for dx in (-1, 0, 1) for dz in (-1, 0, 1) if dx or dz]
-
-    def device(dx, dz):
-        to_z = lax.rem(z + dz + z_n, z_n)
-        return {
-            "gx": lax.rem(gx + dx + gx_n, gx_n),
-            "gz": lax.div(to_z, grp_n),
-            "grp": lax.rem(to_z, grp_n),
-        }
-
-    barrier = pltpu.get_barrier_semaphore()
-    for dx, dz in steps:
-        pl.semaphore_signal(barrier, inc=1, device_id=device(dx, dz), device_id_type=MESH)
-    for c in range(count):
-        strips[0, c] = v_ref[c, :, 0:LANES].T[0:ROWS]
-        strips[1, c] = v_ref[c, :, cx - LANES : cx].T[LANES - ROWS : LANES]
-    pl.semaphore_wait(barrier, len(steps))
-    edge_x = {1: pl.ds(cx - LANES, LANES), -1: pl.ds(0, LANES), 0: pl.ds(0, cx)}
-    edge_z = {1: pl.ds(cz - ROWS, ROWS), -1: pl.ds(0, ROWS)}
-    copies = []
-    for index, (dx, dz) in enumerate(steps):
-        side_x, side_z = int(dx > 0), int(dz > 0)
-        if dz == 0:
-            source, target = strips.at[side_x], xh_ref.at[side_x]
-        else:
-            source = v_ref.at[:, edge_z[dz], edge_x[dx]]
-            target = zh_ref.at[side_z] if dx == 0 else corner_ref.at[2 * side_z + side_x]
-        copies.append(
-            pltpu.make_async_remote_copy(
-                src_ref=source,
-                dst_ref=target,
-                send_sem=send_sem.at[index],
-                recv_sem=recv_sem.at[index],
-                device_id=device(dx, dz),
-                device_id_type=MESH,
-            )
-        )
-    for copy in copies:
-        copy.start()
-    for copy in copies:
-        copy.wait()
-
-
-def halos(velocity, sizes):
-    count, cz, cx = velocity.shape
-    vmem = pl.BlockSpec(memory_space=pltpu.VMEM)
-    return pl.pallas_call(
-        functools.partial(halo_kernel, sizes),
-        out_shape=(
-            jax.ShapeDtypeStruct((2, count, ROWS, cx), f32),
-            jax.ShapeDtypeStruct((2, count, ROWS, cz), f32),
-            jax.ShapeDtypeStruct((4, count, ROWS, LANES), f32),
-        ),
-        in_specs=[vmem],
-        out_specs=(vmem, vmem, vmem),
-        scratch_shapes=[
-            pltpu.VMEM((2, count, ROWS, cz), f32),
-            pltpu.SemaphoreType.DMA((8,)),
-            pltpu.SemaphoreType.DMA((8,)),
-        ],
-        compiler_params=pltpu.CompilerParams(collective_id=0, has_side_effects=True),
-        name="halo",
-    )(velocity)
-
-
-def step_kernel(v_ref, zh_ref, xh_ref, corner_ref, slab_ref, shear_ref, out_ref, start, first, second):
-    p = pl.program_id(0)
-    slab, shear = slab_ref[p], shear_ref[p]
-    _, _, cz, cx = v_ref.shape
+def step_plane(p, planes, v_ref, zh_ref, xh_ref, corner_ref, slab, shear, out_ref, start, first, second):
+    _, cz, cx = v_ref.shape
     top = 2 * ROWS
     lane = lax.broadcasted_iota(jnp.int32, (ROWS, LANES), 1)
     width = cx + LANES
     for c in range(3):
-        start[c, top : top + cz, 0:cx] = v_ref[c, 0]
+        start[c, top : top + cz, 0:cx] = v_ref[c * planes + p]
         strip = jnp.concatenate(
-            [xh_ref[0, c, 0], jnp.zeros((LANES - 2 * ROWS, cz), f32), xh_ref[1, c, 0]], axis=0
+            [
+                xh_ref[0, c * planes + p],
+                jnp.zeros((LANES - 2 * ROWS, cz), f32),
+                xh_ref[1, c * planes + p],
+            ], axis=0
         )
         start[c, top : top + cz, cx:width] = strip.T
         for side, row in ((1, top - ROWS), (0, top + cz)):
-            start[c, row : row + ROWS, 0:cx] = zh_ref[side, c, 0]
+            start[c, row : row + ROWS, 0:cx] = zh_ref[side, c * planes + p]
             start[c, row : row + ROWS, cx:width] = jnp.where(
-                lane < LANES // 2, corner_ref[2 * side, c, 0], corner_ref[2 * side + 1, c, 0]
+                lane < LANES // 2,
+                corner_ref[2 * side, c * planes + p],
+                corner_ref[2 * side + 1, c * planes + p],
             )
 
     def block(source, row):
@@ -171,47 +104,22 @@
             value = start[c, row : row + ROWS, :] * (1.0 / 3.0) + (2.0 / 3.0) * (
                 middle[c] + time_step * rates[c]
             )
-            out_ref[c, 0, row - top : row - top + ROWS, :] = value[:, 0:cx]
-
-
-def advance(velocity, slab, shear, sizes):
-    three, planes, cz, cx = velocity.shape
-    zh, xh, corner = halos(velocity.reshape(three * planes, cz, cx), sizes)
-    smem = pl.BlockSpec(memory_space=pltpu.SMEM)
-    main = pl.BlockSpec((3, 1, cz, cx), lambda p: (0, p, 0, 0))
-
-    def edge(sides, lanes):
-        return pl.BlockSpec((sides, 3, 1, ROWS, lanes), lambda p: (0, 0, p, 0, 0))
-
-    return pl.pallas_call(
-        step_kernel,
-        grid=(planes,),
-        out_shape=jax.ShapeDtypeStruct(velocity.shape, f32),
-        in_specs=[main, edge(2, cx), edge(2, cz), edge(4, LANES), smem, smem],
-        out_specs=main,
-        scratch_shapes=[pltpu.VMEM((3, cz + 4 * ROWS, cx + LANES), f32)] * 3,
-        name="step",
-    )(
-        velocity,
-        zh.reshape(2, three, planes, ROWS, cx),
-        xh.reshape(2, three, planes, ROWS, cz),
-        corner.reshape(4, three, planes, ROWS, LANES),
-        slab,
-        shear,
-    )
+            out_ref[c * planes + p, row - top : row - top + ROWS, :] = value[:, 0:cx]
 
 
 def filter_kernel(
-    sizes, planes, adv_ref, counts_ref, txh_hbm, txl_hbm, tzh_ref, tzl_ref, tth_ref, ttl_ref, gath,
+    sizes, planes, v_ref, slab_ref, shear_ref, counts_ref, txh_hbm, txl_hbm, tzh_ref, tzl_ref, tth_ref,
+    ttl_ref, gath, adv_ref, strips, zh_ref, xh_ref, corner_ref, start, first_ref, second_ref,
     high, low, txh, txl, part_send, part_keep, part_recv, y_send, y_recv, z_send, z_recv, z_out,
     table_sem, ps_sem, pr_sem, ys_sem, yr_sem, zs_sem, zr_sem, os_sem, gr_sem, gy_sem, gp_sem,
+    hs_sem, hr_sem,
 ):
     gx_n, gz_n, grp_n = sizes
     z_n = gz_n * grp_n
     y_n = gx_n // 2
     chunks, total_units, _, lanes = gath.shape
     units = total_units // gx_n
-    _, cz, cx = adv_ref.shape
+    count, cz, cx = adv_ref.shape
     gx = lax.axis_index("gx")
     z = lax.axis_index("gz") * grp_n + lax.axis_index("grp")
     y, core = lax.div(gx, 2), lax.rem(gx, 2)
@@ -233,6 +141,17 @@
     friends = [at_x(y, other)]
     friends += [at_x(lax.rem(y + d, y_n), core) for d in range(1, y_n)]
     friends += [at_z(lax.rem(z + d, z_n)) for d in range(1, z_n)]
+    steps = [(dx, dz) for dx in (-1, 0, 1) for dz in (-1, 0, 1) if dx or dz]
+
+    def near(dx, dz):
+        to_z = lax.rem(z + dz + z_n, z_n)
+        return {
+            "gx": lax.rem(gx + dx + gx_n, gx_n),
+            "gz": lax.div(to_z, grp_n),
+            "grp": lax.rem(to_z, grp_n),
+        }
+
+    friends += [near(dx, dz) for dx, dz in steps]
     for friend in friends:
         pl.semaphore_signal(barrier, inc=1, device_id=friend, device_id_type=MESH)
 
@@ -244,12 +163,36 @@
     for copy in tables:
         copy.start()
 
+    for c in range(count):
+        strips[0, c] = v_ref[c, :, 0:LANES].T[0:ROWS]
+        strips[1, c] = v_ref[c, :, cx - LANES : cx].T[LANES - ROWS : LANES]
+    pl.semaphore_wait(barrier, len(friends))
+    edge_x = {1: pl.ds(cx - LANES, LANES), -1: pl.ds(0, LANES), 0: pl.ds(0, cx)}
+    edge_z = {1: pl.ds(cz - ROWS, ROWS), -1: pl.ds(0, ROWS)}
+    edges = []
+    for index, (dx, dz) in enumerate(steps):
+        side_x, side_z = int(dx > 0), int(dz > 0)
+        if dz == 0:
+            source, target = strips.at[side_x], xh_ref.at[side_x]
+        else:
+            source = v_ref.at[:, edge_z[dz], edge_x[dx]]
+            target = zh_ref.at[side_z] if dx == 0 else corner_ref.at[2 * side_z + side_x]
+        edges.append(remote(source, target, hs_sem.at[index], hr_sem.at[index], near(dx, dz)))
+    for copy in edges:
+        copy.start()
+    for copy in edges:
+        copy.wait()
+
     def put(unit, values):
         h, l = split(values)
         high[unit] = h
         low[unit] = l
 
     def prepare(p, carry):
+        step_plane(
+            p, planes, v_ref, zh_ref, xh_ref, corner_ref, slab_ref[p], shear_ref[p], adv_ref, start,
+            first_ref, second_ref,
+        )
         parts = [adv_ref[i * planes + p] for i in range(3)]
         for i in range(3):
             put(p * FIELDS + i, parts[i])
@@ -384,12 +327,8 @@
                 share(h, slot, d, k).start()
 
     order = list(range(1, y_n)) + [0]
-    first = True
     for d in order:
         analyse(2 * lax.rem(y + d, y_n) + other, part_send, d)
-        if first:
-            pl.semaphore_wait(barrier, len(friends))
-            first = False
         for h in range(chunks):
             to_partner(h, d).start()
         analyse(2 * lax.rem(y + d, y_n) + core, part_keep, d)
@@ -466,12 +405,12 @@
         out_ref[q, 0] = filtered[3 + q] - filtered[a] * filtered[b]
 
 
-def filtered_stress(advanced, mode_counts, sizes):
+def filtered_stress(velocity, slab, shear, mode_counts, sizes):
     gx_n, gz_n, grp_n = sizes
     z_n = gz_n * grp_n
     y_n = gx_n // 2
-    count, cz, cx = advanced.shape
-    planes = count // 3
+    three, planes, cz, cx = velocity.shape
+    count = three * planes
     units = -(-FIELDS * planes // gx_n)
     assert gx_n % 2 == 0 and units <= z_n
     txh, txl = (jnp.asarray(t) for t in split_table(wave_table(cx * gx_n)))
@@ -485,12 +424,21 @@
     total = gx_n * units
     chunks = 2
     lanes = MODES // chunks
-    gathered = pl.pallas_call(
+    smem = pl.BlockSpec(memory_space=pltpu.SMEM)
+    gathered, advanced = pl.pallas_call(
         functools.partial(filter_kernel, sizes, planes),
-        out_shape=jax.ShapeDtypeStruct((chunks, total, cz, lanes), f32),
-        in_specs=[vmem, pl.BlockSpec(memory_space=pltpu.SMEM), anywhere, anywhere, vmem, vmem, vmem, vmem],
-        out_specs=vmem,
+        out_shape=(
+            jax.ShapeDtypeStruct((chunks, total, cz, lanes), f32),
+            jax.ShapeDtypeStruct((count, cz, cx), f32),
+        ),
+        in_specs=[vmem, smem, smem, smem, anywhere, anywhere, vmem, vmem, vmem, vmem],
+        out_specs=(vmem, vmem),
         scratch_shapes=[
+            pltpu.VMEM((2, count, ROWS, cz), f32),
+            pltpu.VMEM((2, count, ROWS, cx), f32),
+            pltpu.VMEM((2, count, ROWS, cz), f32),
+            pltpu.VMEM((4, count, ROWS, LANES), f32),
+            *[pltpu.VMEM((3, cz + 4 * ROWS, cx + LANES), f32)] * 3,
             pltpu.VMEM((total, cz, cx), bf16),
             pltpu.VMEM((total, cz, cx), bf16),
             pltpu.VMEM((cx, MODES), bf16),
@@ -514,11 +462,13 @@
             dma((chunks, total)),
             dma((chunks, others, units)),
             dma((chunks, y_n, units)),
+            dma((8,)),
+            dma((8,)),
         ],
-        compiler_params=pltpu.CompilerParams(collective_id=1, has_side_effects=True),
+        compiler_params=pltpu.CompilerParams(collective_id=0, has_side_effects=True),
         name="filter",
-    )(advanced, mode_counts, txh, txl, *(jnp.asarray(t) for t in (tzh, tzl, tth, ttl)))
-    return pl.pallas_call(
+    )(velocity.reshape(count, cz, cx), slab, shear, mode_counts, txh, txl, *(jnp.asarray(t) for t in (tzh, tzl, tth, ttl)))
+    stress = pl.pallas_call(
         synthesis_kernel,
         grid=(planes,),
         out_shape=jax.ShapeDtypeStruct((6, planes, cz, cx), f32),
@@ -529,13 +479,11 @@
         scratch_shapes=[pltpu.VMEM((cx, MODES), bf16), pltpu.VMEM((cx, MODES), bf16), dma((2,))],
         name="synthesis",
     )(gathered, txh, txl)
+    return advanced.reshape(velocity.shape), stress
 
 
 def local(sizes, velocity, slab, shear, mode_counts):
-    three, planes, cz, cx = velocity.shape
-    advanced = advance(velocity, slab, shear, sizes)
-    stress = filtered_stress(advanced.reshape(three * planes, cz, cx), mode_counts, sizes)
-    return advanced, stress
+    return filtered_stress(velocity, slab, shear, mode_counts, sizes)
 
 
 def solution(mesh):

time: 79.1 us -> 75.9 us (0.960)
  Pallas kernels: 76.6 us -> 72.7 us
  local copies, waits for them, and re-layouts: 1.34 us -> 2.36 us
    pallas_call x2 -> x0, Pallas kernels: 25.1 us -> none  [the longest x1 17.5 us: halos(): pl.pallas_call(functools.partial(halo_kernel, sizes), out_shape=(jax.Shap...]
    pallas_call x1, Pallas kernels: 45.7 us -> 66.8 us  [filtered_stress(): pl.pallas_call(functools.partial(filter_kernel, sizes, planes), out_shape...]
    unnamed x1 -> x4, local copies, waits for them, and re-layouts: 1.34 us -> 2.36 us
where the time goes in v5:
time: 75.9 us; the launch traced here: 75.7 us
  Pallas kernels  72.7 us (96%)
  local copies, waits for them, and re-layouts  2.36 us (3%)
    pallas_call x1, Pallas kernels, filtered_stress(): pl.pallas_call(functools.partial(filter_kernel, sizes, planes), out_shape...  66.8 us
    pallas_call x1, Pallas kernels, filtered_stress(): pl.pallas_call(synthesis_kernel, grid=(planes,), out_shape=jax.ShapeDtype...  5.84 us
    unnamed x4, local copies, waits for them, and re-layouts  2.36 us

profile of v5, /device:TPU:0, one launch (start us, length us, event | category | flops | bytes accessed | tf_op | source)
XLA Modules:
  0.0 75.7 jit_solution(6934923226415714175)
XLA Ops:
  0.6 1.3 %copy.12.counts_ref = s32[3,2]{1,0:T(4,128)} copy(s32[3,2]{0,1:T(2,128)} %param.13) | data formatting | bytes 48 | tf_op args[3]
  2.0 66.8 %filter.1 = (f32[2,28,64,128]{3,2,1,0:T(8,128)}, f32[9,64,512]{2,1,0:T(8,128)}) custom-call(f32[9,64,512]{2,1,0:T(8,128)} %bitcast.3, f32[3]{0:T(128)} %slab_ref.1, f32[3]{0:T(128)} %shear_ref.1, s32[3,2]{1,0:T(4,128)} %copy.12.counts_ref, bf16[2048,256]{1,0:T(8,128)(2,1)} %constant.12.clone.txh_hbm, bf16[2048,256]{1,0:T(8,128)(2,1)} %constant.13.clone.txl_hbm, ...), custom_call_target="tpu_custom_call" | custom-call | tf_op jit(solution)/shard_map/filter/pallas_call | solution.py:428
  68.8 0.0 copy-start
  68.8 5.8 %synthesis.1 = f32[6,3,64,512]{3,2,1,0:T(8,128)} custom-call(f32[2,28,64,128]{3,2,1,0:T(8,128)} %get-tuple-element.5.gath_ref, bf16[2048,256]{1,0:T(8,128)(2,1)} %constant.12.clone.txh_hbm, bf16[2048,256]{1,0:T(8,128)(2,1)} %constant.13.clone.txl_hbm), custom_call_target="tpu_custom_call" | custom-call | tf_op jit(solution)/shard_map/synthesis/pallas_call | solution.py:471
  74.7 0.0 copy-done
  74.7 1.0 %copy.14 = f32[3,3,64,512]{3,2,1,0:T(8,128)} copy(f32[3,3,64,512]{3,2,1,0:T(8,128)S(1)} %bitcast.2) | data formatting | bytes 2359296
Async XLA Ops:
  68.8 5.9 %copy-start = (f32[9,64,512]{2,1,0:T(8,128)S(1)}, f32[9,64,512]{2,1,0:T(8,128)}, u32[]{:S(2)}) copy-start(f32[9,64,512]{2,1,0:T(8,128)} %get-tuple-element.4) | copy-start | bytes 3538948

commit v6 on v5

--- a/solution.py
+++ b/solution.py
@@ -227,11 +227,9 @@
 
     turns = [lax.rem(z + i, units) for i in range(units)]
 
-    def send_y(h, d):
-        to_partner(h, d).wait_recv()
-        for k in turns:
-            y_send[h, d - 1, k] = part_keep[h, d, k] + part_recv[h, d, k]
-            to_y(h, d, k).start()
+    def send_y(h, d, k):
+        y_send[h, d - 1, k] = part_keep[h, d, k] + part_recv[h, d, k]
+        to_y(h, d, k).start()
 
     def forward(h, k):
         return remote(z_send.at[h, k], z_recv.at[h, z], zs_sem.at[h, k], zr_sem.at[h, z], at_z(k))
@@ -243,9 +241,14 @@
 
     def send_z(h):
         to_partner(h, 0).wait_recv()
+        for d in range(1, y_n):
+            if h + 1 < chunks:
+                to_partner(h + 1, d).wait_recv()
         for k in turns:
             for d in range(1, y_n):
                 to_y(h, d, k).wait_recv()
+                if h + 1 < chunks:
+                    send_y(h + 1, d, k)
             total = part_keep[h, 0, k] + part_recv[h, 0, k]
             for d in range(1, y_n):
                 total = total + y_recv[h, d - 1, k]
@@ -333,8 +336,9 @@
             to_partner(h, d).start()
         analyse(2 * lax.rem(y + d, y_n) + core, part_keep, d)
         if d:
-            for h in range(chunks):
-                send_y(h, d)
+            to_partner(0, d).wait_recv()
+            for k in turns:
+                send_y(0, d, k)
     send_z(0)
 
     @pl.when(z < units)

time: 75.9 us -> 75.6 us (level)
  no operation moved by 1% of the time
where the time goes in v6:
time: 75.6 us; the launch traced here: 75.3 us
  Pallas kernels  72.3 us (96%)
  local copies, waits for them, and re-layouts  2.36 us (3%)
    pallas_call x1, Pallas kernels, filtered_stress(): pl.pallas_call(functools.partial(filter_kernel, sizes, planes), out_shape...  66.5 us
    pallas_call x1, Pallas kernels, filtered_stress(): pl.pallas_call(synthesis_kernel, grid=(planes,), out_shape=jax.ShapeDtype...  5.84 us
    unnamed x4, local copies, waits for them, and re-layouts  2.36 us

profile of v6, /device:TPU:0, one launch (start us, length us, event | category | flops | bytes accessed | tf_op | source)
XLA Modules:
  0.0 75.3 jit_solution(13198997546942675158)
XLA Ops:
  0.6 1.3 %copy.12.counts_ref = s32[3,2]{1,0:T(4,128)} copy(s32[3,2]{0,1:T(2,128)} %param.13) | data formatting | bytes 48 | tf_op args[3]
  2.0 66.5 %filter.1 = (f32[2,28,64,128]{3,2,1,0:T(8,128)}, f32[9,64,512]{2,1,0:T(8,128)}) custom-call(f32[9,64,512]{2,1,0:T(8,128)} %bitcast.3, f32[3]{0:T(128)} %slab_ref.1, f32[3]{0:T(128)} %shear_ref.1, s32[3,2]{1,0:T(4,128)} %copy.12.counts_ref, bf16[2048,256]{1,0:T(8,128)(2,1)} %constant.12.clone.txh_hbm, bf16[2048,256]{1,0:T(8,128)(2,1)} %constant.13.clone.txl_hbm, ...), custom_call_target="tpu_custom_call" | custom-call | tf_op jit(solution)/shard_map/filter/pallas_call | solution.py:432
  68.4 0.0 copy-start
  68.4 5.8 %synthesis.1 = f32[6,3,64,512]{3,2,1,0:T(8,128)} custom-call(f32[2,28,64,128]{3,2,1,0:T(8,128)} %get-tuple-element.5.gath_ref, bf16[2048,256]{1,0:T(8,128)(2,1)} %constant.12.clone.txh_hbm, bf16[2048,256]{1,0:T(8,128)(2,1)} %constant.13.clone.txl_hbm), custom_call_target="tpu_custom_call" | custom-call | tf_op jit(solution)/shard_map/synthesis/pallas_call | solution.py:475
  74.3 0.0 copy-done
  74.3 1.0 %copy.14 = f32[3,3,64,512]{3,2,1,0:T(8,128)} copy(f32[3,3,64,512]{3,2,1,0:T(8,128)S(1)} %bitcast.2) | data formatting | bytes 2359296
Async XLA Ops:
  68.4 5.9 %copy-start = (f32[9,64,512]{2,1,0:T(8,128)S(1)}, f32[9,64,512]{2,1,0:T(8,128)}, u32[]{:S(2)}) copy-start(f32[9,64,512]{2,1,0:T(8,128)} %get-tuple-element.4) | copy-start | bytes 3538948
